TPU v7x, 128 devices: a whole 4x4x4 slice. The times are simulated.
128 devices in a mesh: leaf: 128 (over x, y, z, core).
Axes of the slice: x: 4, y: 4, z: 4, core: 2. Of those that a mesh axis runs over, the one named last changes fastest.
Arguments:
- x_vecs: bfloat16 [16, 1048576], P(None, 'leaf'), may hold values from -6 to 6
- leaf_basis: bfloat16 [16384, 4096], P('leaf'), may hold values from -0.75 to 0.75
- near_blocks: bfloat16 [16384, 12288], P('leaf'), may hold values from -0.4375 to 0.4375
- local_edges: float32 [32512, 4096], P('leaf'), may hold values from -0.5 to 0.5
- top_edges: float32 [128, 6, 4096], P('leaf'), may hold values from -1 to 1, as said below
- top_couple: float32 [128, 7, 4096], P('leaf'), may hold values from -3 to 3, as said below
- couple_blocks: bfloat16 [65536, 4096], P('leaf'), may hold values from -0.75 to 0.75
- couple_src: int32 [65536], P('leaf'), may hold values from 0 to 127
- couple_owner: int32 [65536, 1], P('leaf'), may hold values from 0 to 127; in each aligned block of 512 rows (0 to 511, 512 to 1023, ...) at most 8 rows name the same one
- couple_dst: int32 [65536], P('leaf'), may hold values from 0 to 127
Outputs:
- y_vecs: float32 [16, 1048576], P(None, 'leaf')
Inputs may be any that keep to these rules, and one draw needn't show every extreme that they name: `couple_owner`: the rows of one device name each owner at most 8 times, a bound that some block reaches. top_edges[o, b] belongs to the level-b cluster that holds device o and is the same for all devices of that cluster. top_couple[o, b] belongs to the level-b cluster that holds device o and is the same for all devices of that cluster.
All inputs are finite; a program needn't handle non-finite values.
Results may differ from a plain program's by a relative error of at most 0.0044.
Values may be sent and summed in bfloat16 or wider, within the bound.
No kernel may reach another device: no remote copies, remote signals or barrier semaphores. Data moves between devices by JAX's collectives and lax.ppermute only.
A program may use at most 128 MiB of HBM per device.

v0:
```python
import jax
import jax.numpy as jnp
from jax import lax
from jax.experimental import pallas as pl
from jax.experimental.pallas import tpu as pltpu
from jax.sharding import PartitionSpec as P

LEAF = 64
RANK = 64
NV = 16
LEAF_DEV = 128
PEERS = 128
LEVELS = 7
SLOTS = 8
TILES = SLOTS + 2
PAIR_ROWS = 512
EDGE_ROWS = 254
FLAT = 4096
HALF = 64
VMEM_LIMIT = 60 * 1024 * 1024

LEVEL_BASE = {128: 0, 64: 64, 32: 96, 16: 112, 8: 120, 4: 124, 2: 126}

f32 = jnp.float32
bf16 = jnp.bfloat16


def low_lanes(rows):
    return lax.broadcasted_iota(jnp.int32, (rows, 128), 1) < HALF


def half_masks(rows):
    low = low_lanes(rows).astype(f32)
    return low.astype(bf16), (1.0 - low).astype(bf16)


def swap(value):
    return pltpu.roll(value, HALF, 1)


def join(first, second):
    return jnp.where(low_lanes(first.shape[0]), first, swap(second))


def split(value):
    high = value.astype(bf16)
    return high, (value - high.astype(f32)).astype(bf16)


def mm(left, right):
    return jnp.dot(left, right, preferred_element_type=f32)


def mmt(left, right):
    return lax.dot_general(left, right, (((1,), (1,)), ((), ())), preferred_element_type=f32)


def paired(stage, group, load_first, load_second):
    low = low_lanes(group)
    for j in range(32):
        first = load_first(j)
        second = load_second(j)
        stage[pl.ds(2 * j * group, group), :] = jnp.where(low, first, swap(second))
        stage[pl.ds((2 * j + 1) * group, group), :] = jnp.where(low, swap(first), second)


def matrix(stage, group, index):
    return stage[pl.ds(index, 64, stride=group), :]


def lanes(j, start=0):
    return pl.ds(start + j * 128, 128)


def relayout_edges(edges, stage, highs, lows):
    def keep(index, place):
        high, low = split(matrix(stage, 8, index))
        highs[place] = high
        lows[place] = low

    def group(g, _):
        first = jnp.where(
            g < 8, 8 * g, jnp.where(g < 12, 64 + 8 * g, jnp.where(g < 14, 96 + 8 * g, 224))
        )
        gap = jnp.where(g < 8, 64, jnp.where(g < 12, 32, jnp.where(g < 14, 16, 8)))
        first = pl.multiple_of(first, 8)
        second = pl.multiple_of(first + gap, 8)
        paired(
            stage,
            8,
            lambda j: edges[pl.ds(first, 8), lanes(j)],
            lambda j: edges[pl.ds(second, 8), lanes(j)],
        )
        for i in range(8):
            keep(i, 8 * g + i)
        return 0

    lax.fori_loop(0, 15, group, 0)
    paired(
        stage,
        8,
        lambda j: edges[240:248, lanes(j)],
        lambda j: pltpu.roll(edges[240:248, lanes(j)], 4, 0),
    )
    for i in range(4):
        keep(i, 120 + i)
    rows = lax.broadcasted_iota(jnp.int32, (8, 128), 0)

    def last_second(j):
        tile = edges[246:254, lanes(j)]
        return jnp.where(rows < 6, pltpu.roll(tile, 6, 0), pltpu.roll(tile, 7, 0))

    paired(stage, 8, lambda j: edges[246:254, lanes(j)], last_second)
    keep(2, 124)
    keep(3, 125)
    keep(6, 126)


def up_kernel(
    me_ref, src_ref, own_ref, dst_ref, x_ref, basis_hbm, edges_hbm, top_ref, pairs_hbm,
    out_ref, done_ref,
    basis, edges, pairs, stage, vec_a, vec_b, highs, lows, table, rows_at, count, sems,
):
    copies = [
        pltpu.make_async_copy(basis_hbm, basis, sems.at[0]),
        pltpu.make_async_copy(edges_hbm, edges, sems.at[1]),
        pltpu.make_async_copy(pairs_hbm, pairs, sems.at[2]),
    ]
    for copy in copies:
        copy.start()
    low16, high16 = half_masks(16)
    low = low_lanes(16)

    def clear(i, _):
        out_ref[pl.ds(i * 16, 16)] = jnp.zeros((16, 8, 128), bf16)
        return 0

    lax.fori_loop(0, PEERS * TILES // 16, clear, 0)
    rows_at[...] = jnp.zeros_like(rows_at)

    def clear_count(i, _):
        count[i] = 0
        return 0

    lax.fori_loop(0, PEERS, clear_count, 0)

    copies[0].wait()

    def leaf_group(g, _):
        first = pl.multiple_of(16 * g, 16)
        second = pl.multiple_of(64 + 16 * g, 16)
        paired(
            stage,
            16,
            lambda j: basis[pl.ds(first, 16), lanes(j)].astype(f32),
            lambda j: basis[pl.ds(second, 16), lanes(j)].astype(f32),
        )
        for i in range(0, 16, 2):
            weight = jnp.concatenate([matrix(stage, 16, i), matrix(stage, 16, i + 1)], axis=0)
            at = pl.multiple_of(g * 1024 + i * 64, 128)
            left = x_ref[:, pl.ds(at, 128)]
            right = x_ref[:, pl.ds(pl.multiple_of(at + FLAT, 128), 128)]
            stacked = jnp.concatenate(
                [left * low16, right * low16, left * high16, right * high16], axis=0
            )
            found = mm(stacked, weight.astype(bf16))
            for k in range(2):
                pair = jnp.where(low, found[32 * k : 32 * k + 16], found[32 * k + 16 : 32 * k + 32])
                turned = swap(pair)
                t = 16 * g + i + k
                vec_a[t] = pair
                table[t] = jnp.where(low, pair, turned).astype(bf16)
                table[t + 64] = jnp.where(low, turned, pair).astype(bf16)
        return 0

    lax.fori_loop(0, 4, leaf_group, 0)

    copies[1].wait()
    relayout_edges(edges, stage, highs, lows)

    here, there = vec_a, vec_b
    nodes = LEAF_DEV
    while nodes > 2:
        base = LEVEL_BASE[nodes]

        def parent(q, here=here, there=there, base=base):
            p0 = here[2 * q]
            p1 = here[2 * q + 1]
            both = jnp.concatenate(
                [jnp.where(low, p0, swap(p1)), jnp.where(low, swap(p0), p1)], axis=0
            )
            vh, vl = split(both)
            wh = highs[pl.ds(base + 2 * q, 2)].reshape(128, 128)
            wl = lows[pl.ds(base + 2 * q, 2)].reshape(128, 128)
            two = mm(jnp.concatenate([vh, vl], axis=0), wh)
            found = two[:32] + two[32:] + mm(vh, wl)
            there[q] = jnp.where(low, found[:16], found[16:])

        quarter = nodes // 4
        if quarter > 8:

            def block(i, _, parent=parent):
                for k in range(8):
                    parent(8 * i + k)
                return 0

            lax.fori_loop(0, quarter // 8, block, 0)
        else:
            for q in range(quarter):
                parent(q)
        here, there = there, here
        nodes //= 2
    last = here[0]
    both = jnp.concatenate([last, swap(last)], axis=0)[:, :HALF]
    vh, vl = split(both)
    wh = highs[126]
    two = mm(jnp.concatenate([vh, vl], axis=0), wh)
    found = two[:32] + two[32:] + mm(vh, lows[126])
    current = found[:16] + swap(found[16:])

    for j in range(32):
        tile = top_ref[:, lanes(j)]
        stage[pl.ds(16 * j, LEVELS - 1), :] = tile
        stage[pl.ds(16 * j + 8, LEVELS - 1), :] = swap(tile)
    me = me_ref[0]
    for level in range(LEVELS):
        tile = join(current[0:8], current[8:16]).astype(bf16)
        for x in range(2**level, 2 ** (level + 1)):
            out_ref[lax.bitwise_xor(me, x) * TILES + SLOTS] = tile
        if level < LEVELS - 1:
            wh, wl = split(matrix(stage, 8, level))
            vh, vl = split(current[:, :HALF])
            two = mm(jnp.concatenate([vh, vl], axis=0), wh)
            current = two[:16] + two[16:] + mm(vh, wl)

    copies[2].wait()
    lane_ids = lax.broadcasted_iota(jnp.int32, (1, 128), 1)

    def pair_group(g, _):
        first = pl.multiple_of(32 * g, 16)
        second = pl.multiple_of(32 * g + 16, 16)
        paired(
            stage,
            16,
            lambda j: pairs[pl.ds(first, 16), lanes(j)].astype(f32),
            lambda j: pairs[pl.ds(second, 16), lanes(j)].astype(f32),
        )
        for i in range(16):
            weight = matrix(stage, 16, i).astype(bf16)
            listed = [32 * g + i, 32 * g + 16 + i]
            stacked = jnp.concatenate(
                [table[src_ref[listed[0]]] * low16, table[src_ref[listed[1]]] * high16], axis=0
            )
            found = mmt(stacked, weight)
            for k in range(2):
                owner = own_ref[listed[k]]
                rank = count[owner]
                count[owner] = rank + 1
                tile = jnp.concatenate(
                    [found[16 * k : 16 * k + 8], found[16 * k + 8 : 16 * k + 16]], axis=1
                )
                out_ref[owner * TILES + rank] = tile.astype(bf16)
                rows_at[pl.ds(owner * SLOTS + rank, 1), :] = jnp.where(
                    lane_ids == dst_ref[listed[k]], 1.0, 0.0
                )
        return 0

    lax.fori_loop(0, PAIR_ROWS // 32, pair_group, 0)

    def place_rows(o, _):
        out_ref[o * TILES + SLOTS + 1] = rows_at[
            pl.ds(pl.multiple_of(o * SLOTS, 8), 8), :
        ].astype(bf16)
        return 0

    lax.fori_loop(0, PEERS, place_rows, 0, unroll=8)
    done_ref[...] = current[0:8]


def mid_kernel(
    after_ref, xs_ref, xe_ref, near_hbm, basis_hbm, edges_hbm, top_ref,
    near_ref, down_ref, basis_ref, top_out_ref,
    near, basis, edges, stage, stage_two, vec_a, vec_b, highs, lows, sems,
):
    copies = [
        pltpu.make_async_copy(near_hbm, near, sems.at[0]),
        pltpu.make_async_copy(basis_hbm, basis, sems.at[1]),
        pltpu.make_async_copy(edges_hbm, edges, sems.at[2]),
    ]
    for copy in copies:
        copy.start()
    low16, _ = half_masks(16)
    low64, high64 = half_masks(64)
    flow = low_lanes(128)

    copies[0].wait()

    def near_group(g, _):
        first = pl.multiple_of(16 * g, 16)
        rows = pl.ds(first, 16)
        paired(
            stage,
            16,
            lambda j: near[rows, lanes(j)].astype(f32),
            lambda j: near[rows, lanes(j, FLAT)].astype(f32),
        )
        for j in range(32):
            tile = near[rows, lanes(j, 2 * FLAT)].astype(f32)
            stage_two[pl.ds(32 * j, 16), :] = tile
            stage_two[pl.ds(32 * j + 16, 16), :] = swap(tile)
        for i in range(0, 16, 2):
            at = pl.multiple_of(g * 1024 + i * 64, 128)
            after = pl.multiple_of(at + 128, 128)
            found = []
            for k, ref in enumerate((xs_ref, xe_ref)):
                weight = jnp.concatenate(
                    [matrix(stage, 16, i + k), matrix(stage_two, 16, i + k)], axis=1
                ).astype(bf16)
                vec = jnp.concatenate(
                    [ref[:, pl.ds(at, 128)], ref[:, pl.ds(after, 128)] * low16], axis=1
                )
                found.append(mmt(vec, weight))
            near_ref[:, pl.ds(at, 128)] = jnp.concatenate(found, axis=1)
        return 0

    lax.fori_loop(0, 8, near_group, 0)

    copies[1].wait()
    even = (lax.broadcasted_iota(jnp.int32, (16, 128), 0) % 2) == 0

    def basis_group(g, _):
        rows = pl.ds(pl.multiple_of(16 * g, 16), 16)
        for j in range(32):
            tile = basis[rows, lanes(j)].astype(f32)
            turned = swap(tile)
            stage[pl.ds(32 * j, 16), :] = jnp.where(even, tile, turned)
            stage[pl.ds(32 * j + 16, 16), :] = jnp.where(even, turned, tile)
        for i in range(16):
            at = pl.multiple_of(g * 1024 + i * 64, 64)
            value = matrix(stage, 16, i).astype(bf16)
            basis_ref[pl.ds(at, 64), :] = value * (high64 if i % 2 else low64)
        return 0

    lax.fori_loop(0, 8, basis_group, 0)

    copies[2].wait()
    relayout_edges(edges, stage, highs, lows)
    vec_a[0] = highs[126].astype(f32) + lows[126].astype(f32)
    here, there = vec_a, vec_b
    nodes = 4
    while nodes <= LEAF_DEV:
        base = LEVEL_BASE[nodes]

        def children(q, here=here, there=there, base=base, final=nodes == LEAF_DEV):
            ph, plow = split(here[q])
            rh = jnp.concatenate([ph * low64, ph * high64], axis=0)
            rl = jnp.concatenate([plow * low64, plow * high64], axis=0)
            wh = highs[pl.ds(base + 2 * q, 2)].reshape(128, 128)
            wl = lows[pl.ds(base + 2 * q, 2)].reshape(128, 128)
            found = mm(wh, rh) + mm(wl, rh) + mm(wh, rl)
            if not final:
                there[2 * q] = found[:64]
                there[2 * q + 1] = found[64:]
            else:
                high = found.astype(bf16).astype(f32)
                rest = found - high
                at = pl.multiple_of(q * 128, 128)
                down_ref[pl.ds(at, 128), :] = jnp.where(flow, high, swap(rest)).astype(bf16)
                at = pl.multiple_of(q * 128 + FLAT, 128)
                down_ref[pl.ds(at, 128), :] = jnp.where(flow, swap(high), rest).astype(bf16)

        quarter = nodes // 4
        if quarter > 4:

            def block(i, _, children=children):
                for k in range(4):
                    children(4 * i + k)
                return 0

            lax.fori_loop(0, quarter // 4, block, 0)
        else:
            for q in range(quarter):
                children(q)
        here, there = there, here
        nodes *= 2

    paired(stage, 8, lambda j: top_ref[0:8, lanes(j)], lambda j: top_ref[8:16, lanes(j)])
    low = low_lanes(64)
    chain = None
    for level in range(LEVELS):
        value = matrix(stage, 8, level)
        if chain is None:
            found = value
        else:
            wh, wl = split(value)
            vh, vl = split(chain[:, :HALF])
            found = mm(vh, wh) + mm(vl, wh) + mm(vh, wl)
        chain = found
        high = found.astype(bf16).astype(f32)
        top_out_ref[level] = jnp.where(low, swap(high), found - high).astype(bf16)


def down_kernel(
    me_ref, got_ref, near_ref, down_ref, basis_ref, top_ref,
    out_ref,
    values, target, far,
):
    low8 = low_lanes(8)
    low16, _ = half_masks(16)

    def unpack(o, _):
        for s in range(SLOTS):
            at = pl.multiple_of((o * SLOTS + s) * 8, 8)
            values[pl.ds(at, 8), :] = got_ref[o * TILES + s].astype(f32)
        at = pl.multiple_of(o * SLOTS, 8)
        target[pl.ds(at, 8), :] = got_ref[o * TILES + SLOTS + 1].astype(f32)
        return 0

    lax.fori_loop(0, PEERS, unpack, 0, unroll=4)
    landing = jnp.concatenate(
        [target[128 * i : 128 * i + 128, :].T for i in range(SLOTS)], axis=1
    ).astype(bf16)
    for u in range(8):
        chosen = values[pl.ds(u, PEERS * SLOTS, stride=8), :].astype(bf16)
        far[128 * u : 128 * u + 128, :] = mm(landing, chosen)

    def doubled(tile):
        turned = swap(tile)
        both = jnp.concatenate(
            [jnp.where(low8, tile, turned), jnp.where(low8, turned, tile)], axis=0
        )
        return both

    def halves(value):
        high, rest = split(value)
        return jnp.concatenate([high, rest * low16], axis=0)

    me = me_ref[0]
    total = jnp.zeros((2 * NV, HALF), f32)
    for level in range(LEVELS):
        parts = []
        for x in range(2**level, 2 ** (level + 1)):
            tile = got_ref[lax.bitwise_xor(me, x) * TILES + SLOTS].astype(f32)
            if len(parts) < 4:
                parts.append(tile)
            else:
                parts[x % 4] = parts[x % 4] + tile
        tile = parts[0]
        for part in parts[1:]:
            tile = tile + part
        total = total + mmt(halves(doubled(tile)), top_ref[level])
    root = total[:NV] + total[NV:]
    root = halves(jnp.concatenate([root, root], axis=1))

    def leaf_pair(i):
        at = pl.multiple_of(i * 128, 128)
        two = mmt(root, down_ref[pl.ds(at, 128), :])
        f0 = far[pl.ds(2 * i, 8, stride=128), :]
        f1 = far[pl.ds(2 * i + 1, 8, stride=128), :]
        gathered = jnp.concatenate(
            [jnp.where(low8, f0, swap(f1)), jnp.where(low8, swap(f0), f1)], axis=0
        )
        hat = (two[:NV] + two[NV:] + gathered).astype(bf16)
        out_ref[:, pl.ds(at, 128)] = mmt(hat, basis_ref[pl.ds(at, 128), :]) + near_ref[
            :, pl.ds(at, 128)
        ]

    def leaf_block(i, _):
        for k in range(8):
            leaf_pair(8 * i + k)
        return 0

    lax.fori_loop(0, 8, leaf_block, 0)


def vmem():
    return pl.BlockSpec(memory_space=pltpu.VMEM)


def smem():
    return pl.BlockSpec(memory_space=pltpu.SMEM)


def hbm():
    return pl.BlockSpec(memory_space=pl.ANY)


def params():
    return pltpu.CompilerParams(vmem_limit_bytes=VMEM_LIMIT)


def shape(dims, dtype):
    return jax.ShapeDtypeStruct(dims, dtype)


def run_up(me, src, own, dst, x_vecs, basis, edges, top_edges, pairs):
    return pl.pallas_call(
        up_kernel,
        name="up",
        out_shape=(shape((PEERS * TILES, 8, 128), bf16), shape((8, 128), f32)),
        in_specs=[smem(), smem(), smem(), smem(), vmem(), hbm(), hbm(), vmem(), hbm()],
        out_specs=(vmem(), vmem()),
        scratch_shapes=[
            pltpu.VMEM((LEAF_DEV, FLAT), bf16),
            pltpu.VMEM((EDGE_ROWS, FLAT), f32),
            pltpu.VMEM((PAIR_ROWS, FLAT), bf16),
            pltpu.VMEM((1024, 128), f32),
            pltpu.VMEM((64, NV, 128), f32),
            pltpu.VMEM((64, NV, 128), f32),
            pltpu.VMEM((128, 64, 128), bf16),
            pltpu.VMEM((128, 64, 128), bf16),
            pltpu.VMEM((LEAF_DEV, NV, 128), bf16),
            pltpu.VMEM((PEERS * SLOTS, 128), f32),
            pltpu.SMEM((PEERS,), jnp.int32),
            pltpu.SemaphoreType.DMA((3,)),
        ],
        compiler_params=params(),
        cost_estimate=pl.CostEstimate(
            flops=10**9, bytes_accessed=12 * 10**6, transcendentals=0
        ),
    )(me, src, own, dst, x_vecs, basis, edges, top_edges, pairs)


def run_mid(after, xs, xe, near, basis, edges, top):
    return pl.pallas_call(
        mid_kernel,
        name="mid",
        out_shape=(
            shape((NV, LEAF_DEV * LEAF), f32),
            shape((LEAF_DEV * RANK, 128), bf16),
            shape((LEAF_DEV * LEAF, 128), bf16),
            shape((LEVELS, RANK, 128), bf16),
        ),
        in_specs=[vmem(), vmem(), vmem(), hbm(), hbm(), hbm(), vmem()],
        out_specs=(vmem(), vmem(), vmem(), vmem()),
        scratch_shapes=[
            pltpu.VMEM((LEAF_DEV, 3 * FLAT), bf16),
            pltpu.VMEM((LEAF_DEV, FLAT), bf16),
            pltpu.VMEM((EDGE_ROWS, FLAT), f32),
            pltpu.VMEM((1024, 128), f32),
            pltpu.VMEM((1024, 128), f32),
            pltpu.VMEM((64, 64, 128), f32),
            pltpu.VMEM((64, 64, 128), f32),
            pltpu.VMEM((128, 64, 128), bf16),
            pltpu.VMEM((128, 64, 128), bf16),
            pltpu.SemaphoreType.DMA((3,)),
        ],
        compiler_params=params(),
        cost_estimate=pl.CostEstimate(
            flops=10**9, bytes_accessed=14 * 10**6, transcendentals=0
        ),
    )(after, xs, xe, near, basis, edges, top)


def run_down(me, got, near, down, basis, top):
    return pl.pallas_call(
        down_kernel,
        name="down",
        out_shape=shape((NV, LEAF_DEV * LEAF), f32),
        in_specs=[smem(), vmem(), vmem(), vmem(), vmem(), vmem()],
        out_specs=vmem(),
        scratch_shapes=[
            pltpu.VMEM((PEERS * SLOTS * 8, 128), f32),
            pltpu.VMEM((PEERS * SLOTS, 128), f32),
            pltpu.VMEM((8 * LEAF_DEV, 128), f32),
        ],
        compiler_params=params(),
        cost_estimate=pl.CostEstimate(
            flops=10**9, bytes_accessed=8 * 10**6, transcendentals=0
        ),
    )(me, got, near, down, basis, top)


def shards(
    x_vecs,
    leaf_basis,
    near_blocks,
    local_edges,
    top_edges,
    top_couple,
    couple_blocks,
    couple_src,
    couple_owner,
    couple_dst,
):
    ahead = [(i, (i + 1) % PEERS) for i in range(PEERS)]
    back = [(target, source) for source, target in ahead]
    before = lax.ppermute(x_vecs[:, -LEAF:], "leaf", ahead)
    following = lax.ppermute(x_vecs[:, :LEAF], "leaf", back)
    me = lax.axis_index("leaf").astype(jnp.int32).reshape(1)
    outgoing, after = run_up(
        me, couple_src, couple_owner.reshape(PAIR_ROWS), couple_dst, x_vecs, leaf_basis,
        local_edges, top_edges[0], couple_blocks,
    )
    got = lax.all_to_all(
        outgoing.reshape(PEERS, TILES * 8, 128), "leaf", split_axis=0, concat_axis=0, tiled=True
    ).reshape(PEERS * TILES, 8, 128)
    fill = jnp.zeros((NV, LEAF), bf16)
    xs = jnp.concatenate([before, x_vecs, following], axis=1)
    xe = jnp.concatenate([x_vecs, following, fill], axis=1)
    row = jnp.zeros((1, FLAT), f32)
    top = jnp.concatenate([top_edges[0], row, row, top_couple[0], row], axis=0)
    near, down, basis, tops = run_mid(
        after, xs, xe, near_blocks, leaf_basis, local_edges, top
    )
    return run_down(me, got, near, down, basis, tops)


def solution(mesh):
    return jax.shard_map(
        shards,
        mesh=mesh,
        in_specs=(
            P(None, "leaf"),
            P("leaf", None),
            P("leaf", None),
            P("leaf", None),
            P("leaf", None, None),
            P("leaf", None, None),
            P("leaf", None),
            P("leaf"),
            P("leaf", None),
            P("leaf"),
        ),
        out_specs=P(None, "leaf"),
        check_vma=False,
    )
```

profile of v0, /device:TPU:0, one launch (start us, length us, event | category | flops | bytes accessed | tf_op | source)
XLA Modules:
  0.0 101.9 jit_solution(3138605748259268600)
XLA Ops:
  0.0 1.6 %copy.16 = f32[1,6,4096]{2,1,0:T(8,128)} copy(f32[1,6,4096]{2,0,1:T(1,128)} %param.14) | data formatting | bytes 196608
  1.6 20.4 %up.1 = (bf16[1280,8,128]{2,1,0:T(8,128)(2,1)}, f32[8,128]{1,0:T(8,128)}) custom-call(s32[1]{0:T(128)} %bitcast.me_ref, s32[512]{0:T(512)} %src_ref.1, s32[512]{0:T(512)} %bitcast.16, s32[512]{0:T(512)} %dst_ref.1, bf16[16,8192]{1,0:T(8,128)(2,1)} %x_ref.1, bf16[128,4096]{1,0:T(8,128)(2,1)} %basis_hbm.3, f32[254,4096]{1,0:T(8,128)} %edges_hbm.3, ...), custom_call_target="tpu_custom_call" | custom-call | flops 1000000000 | bytes 12000000 | tf_op jit(solution)/shard_map/up/pallas_call | solution.py:497
  22.0 0.0 copy-start.1
  22.0 0.0 copy-start.3
  22.1 0.0 copy-start.2
  22.1 11.2 %all-to-all-start = ((bf16[128,80,128]{2,1,0:T(8,128)(2,1)}), bf16[128,80,128]{2,1,0:T(8,128)(2,1)S(1)}, u32[]{:S(2)}, u32[]{:S(2)}) async-start(bf16[128,80,128]{2,1,0:T(8,128)(2,1)} %bitcast.12), calls=%async_computation | async-start | bytes 5242880 | tf_op jit(solution)/shard_map/all_to_all | solution.py:595
  33.2 0.0 copy-done.1
  33.2 0.1 fusion
  33.3 7.1 %collective-permute-start.1 = (bf16[16,64]{1,0:T(8,128)(2,1)S(1)}, bf16[16,64]{1,0:T(8,128)(2,1)S(1)}, u32[]{:S(2)}, u32[]{:S(2)}) collective-permute-start(bf16[16,64]{1,0:T(8,128)(2,1)S(1)} %get-tuple-element.17), channel_id=1, source_target_pairs={{1,0},{2,1},{3,2},{4,3},{5,4},{6,5},{7,6},{8,7},{9,8},{10,9},{11,1... | collective-permute-start | bytes 6152 | tf_op jit(solution)/shard_map/ppermute | solution.py:589
  40.4 0.0 collective-permute-start
  40.4 0.1 pad.3.clone
  40.5 0.1 pad.1.clone
  40.5 0.1 copy.15
  40.6 0.0 copy-done.2
  40.6 0.8 maximum_maximum_fusion.top_ref
  41.4 17.2 %collective-permute-done.1 = bf16[16,64]{1,0:T(8,128)(2,1)S(1)} collective-permute-done((bf16[16,64]{1,0:T(8,128)(2,1)S(1)}, bf16[16,64]{1,0:T(8,128)(2,1)S(1)}, u32[]{:S(2)}, u32[]{:S(2)}) %collective-permute-start.1) | collective-permute-done | bytes 2080 | tf_op jit(solution)/shard_map/ppermute | solution.py:589
  58.6 9.9 %collective-permute-done = bf16[16,64]{1,0:T(8,128)(2,1)S(1)} collective-permute-done((bf16[16,64]{1,0:T(8,128)(2,1)S(1)}, bf16[16,64]{1,0:T(8,128)(2,1)S(1)}, u32[]{:S(2)}, u32[]{:S(2)}) %collective-permute-start) | collective-permute-done | bytes 2080 | tf_op jit(solution)/shard_map/ppermute | solution.py:588
  68.5 0.9 concatenate.12.xs_ref
  69.5 0.8 concatenate.13.xe_ref
  70.2 20.4 %mid.1 = (f32[16,8192]{1,0:T(8,128)}, bf16[8192,128]{1,0:T(8,128)(2,1)}, bf16[8192,128]{1,0:T(8,128)(2,1)}, bf16[7,64,128]{2,1,0:T(8,128)(2,1)}) custom-call(f32[8,128]{1,0:T(8,128)} %get-tuple-element.12.after_ref, bf16[16,8320]{1,0:T(8,128)(2,1)} %concatenate.12.xs_ref, bf16[16,8320]{1,0:T(8,128)(2,1)} %concatenate.13.xe_ref, bf16[128,12288]{1,0:T(8,128)(2,1)} %near_hbm.1, ...), custom_call_target="tpu_custom_call" | custom-call | flops 1000000000 | bytes 14000000 | tf_op jit(solution)/shard_map/mid/pallas_call | solution.py:525
  90.6 0.0 all-to-all-done
  90.7 0.0 copy-start
  90.7 1.5 %copy-done = bf16[128,80,128]{2,1,0:T(8,128)(2,1)} copy-done((bf16[128,80,128]{2,1,0:T(8,128)(2,1)}, bf16[128,80,128]{2,1,0:T(8,128)(2,1)S(1)}, u32[]{:S(2)}) %copy-start) | copy-done | bytes 2621464
  92.2 9.7 %down.1 = f32[16,8192]{1,0:T(8,128)} custom-call(s32[1]{0:T(128)} %bitcast.me_ref, bf16[1280,8,128]{2,1,0:T(8,128)(2,1)} %bitcast.11, f32[16,8192]{1,0:T(8,128)} %get-tuple-element.13.near_ref, bf16[8192,128]{1,0:T(8,128)(2,1)} %get-tuple-element.14.down_ref, bf16[8192,128]{1,0:T(8,128)(2,1)} %get-tuple-element.15.basis_ref, ...), custom_call_target="tpu_custom_call" | custom-call | flops 1000000000 | bytes 8000000 | tf_op jit(solution)/shard_map/down/pallas_call | solution.py:556
  (3 shorter events, 0.0 us)
Async XLA Ops:
  22.0 11.2 %copy-start.1 = (bf16[16,8192]{1,0:T(8,128)(2,1)S(1)}, bf16[16,8192]{1,0:T(8,128)(2,1)}, u32[]{:S(2)}) copy-start(bf16[16,8192]{1,0:T(8,128)(2,1)} %x_ref.1) | copy-start | bytes 786436
  22.0 18.5 %copy-start.3 = (f32[1,7,4096]{2,0,1:T(1,128)S(1)}, f32[1,7,4096]{2,0,1:T(1,128)}, u32[]{:S(2)}) copy-start(f32[1,7,4096]{2,0,1:T(1,128)} %param.15) | copy-start | bytes 344068
  22.1 18.6 %copy-start.2 = (f32[1,6,4096]{2,1,0:T(8,128)S(1)}, f32[1,6,4096]{2,1,0:T(8,128)}, u32[]{:S(2)}) copy-start(f32[1,6,4096]{2,1,0:T(8,128)} %copy.16) | copy-start | bytes 294916
  22.1 68.6 %all-to-all-start = ((bf16[128,80,128]{2,1,0:T(8,128)(2,1)}), bf16[128,80,128]{2,1,0:T(8,128)(2,1)S(1)}, u32[]{:S(2)}, u32[]{:S(2)}) async-start(bf16[128,80,128]{2,1,0:T(8,128)(2,1)} %bitcast.12), calls=%async_computation | async-start | bytes 5242880 | tf_op jit(solution)/shard_map/all_to_all | solution.py:595
  33.3 25.3 %collective-permute-start.1 = (bf16[16,64]{1,0:T(8,128)(2,1)S(1)}, bf16[16,64]{1,0:T(8,128)(2,1)S(1)}, u32[]{:S(2)}, u32[]{:S(2)}) collective-permute-start(bf16[16,64]{1,0:T(8,128)(2,1)S(1)} %get-tuple-element.17), channel_id=1, source_target_pairs={{1,0},{2,1},{3,2},{4,3},{5,4},{6,5},{7,6},{8,7},{9,8},{10,9},{11,1... | collective-permute-start | bytes 6152 | tf_op jit(solution)/shard_map/ppermute | solution.py:589
  40.4 28.1 %collective-permute-start = (bf16[16,64]{1,0:T(8,128)(2,1)S(1)}, bf16[16,64]{1,0:T(8,128)(2,1)S(1)}, u32[]{:S(2)}, u32[]{:S(2)}) collective-permute-start(bf16[16,64]{1,0:T(8,128)(2,1)S(1)} %get-tuple-element.18), channel_id=1, source_target_pairs={{0,1},{1,2},{2,3},{3,4},{4,5},{5,6},{6,7},{7,8},{8,9},{9,10},{10,1... | collective-permute-start | bytes 6152 | tf_op jit(solution)/shard_map/ppermute | solution.py:588
  90.7 1.5 %copy-start = (bf16[128,80,128]{2,1,0:T(8,128)(2,1)}, bf16[128,80,128]{2,1,0:T(8,128)(2,1)S(1)}, u32[]{:S(2)}) copy-start(bf16[128,80,128]{2,1,0:T(8,128)(2,1)S(1)} %all-to-all-done) | copy-start | bytes 7864324
where the time goes:
time: 102 us
  Pallas kernels  50.5 us (50%)
  waiting for transfers between devices  27.1 us (27%)
  starting transfers between devices  18.2 us (18%)
  local copies, waits for them, and re-layouts  5.17 us (5%)
    pallas_call x1, Pallas kernels, run_up(): pl.pallas_call(up_kernel, name='up', out_shape=(shape((PEERS * TILES, 8,...  20.4 us
    pallas_call x1, Pallas kernels, run_mid(): pl.pallas_call(mid_kernel, name='mid', out_shape=(shape((NV, LEAF_DEV * L...  20.4 us
    ppermute x1, waiting for transfers between devices, shards(): following = lax.ppermute(x_vecs[:, :LEAF], 'leaf', back)  17.2 us
    all_to_all x1, starting transfers between devices, shards(): lax.all_to_all(outgoing.reshape(PEERS, TILES * 8, 128), 'leaf', split_axi...  11.2 us
    ppermute x1, waiting for transfers between devices, shards(): before = lax.ppermute(x_vecs[:, -LEAF:], 'leaf', ahead)  9.92 us
    pallas_call x1, Pallas kernels, run_down(): pl.pallas_call(down_kernel, name='down', out_shape=shape((NV, LEAF_DEV *...  9.73 us
    ppermute x1, starting transfers between devices, shards(): following = lax.ppermute(x_vecs[:, :LEAF], 'leaf', back)  7.06 us
    unnamed x10, local copies, waits for them, and re-layouts  3.22 us
  transfers between devices with their start and end apart: 3, of which 2 were waited for; matrix products, arithmetic and copies ran while one was open for 3% of the time, Pallas kernels for 20%

commit v1 on v0

--- a/solution.py
+++ b/solution.py
@@ -17,7 +17,7 @@
 EDGE_ROWS = 254
 FLAT = 4096
 HALF = 64
-VMEM_LIMIT = 60 * 1024 * 1024
+MIB = 1024 * 1024
 
 LEVEL_BASE = {128: 0, 64: 64, 32: 96, 16: 112, 8: 120, 4: 124, 2: 126}
 
@@ -119,7 +119,7 @@
 def up_kernel(
     me_ref, src_ref, own_ref, dst_ref, x_ref, basis_hbm, edges_hbm, top_ref, pairs_hbm,
     out_ref, done_ref,
-    basis, edges, pairs, stage, vec_a, vec_b, highs, lows, table, rows_at, count, sems,
+    basis, edges, pairs, stage, stage_two, vec_a, vec_b, highs, lows, table, rows_at, count, sems,
 ):
     copies = [
         pltpu.make_async_copy(basis_hbm, basis, sems.at[0]),
@@ -218,17 +218,17 @@
     found = two[:32] + two[32:] + mm(vh, lows[126])
     current = found[:16] + swap(found[16:])
 
-    for j in range(32):
-        tile = top_ref[:, lanes(j)]
-        stage[pl.ds(16 * j, LEVELS - 1), :] = tile
-        stage[pl.ds(16 * j + 8, LEVELS - 1), :] = swap(tile)
+    for level in range(LEVELS - 1):
+        tile = top_ref[32 * level : 32 * level + 32, :]
+        stage[pl.ds(64 * level, 32, stride=2), :] = tile
+        stage[pl.ds(64 * level + 1, 32, stride=2), :] = swap(tile)
     me = me_ref[0]
     for level in range(LEVELS):
         tile = join(current[0:8], current[8:16]).astype(bf16)
         for x in range(2**level, 2 ** (level + 1)):
             out_ref[lax.bitwise_xor(me, x) * TILES + SLOTS] = tile
         if level < LEVELS - 1:
-            wh, wl = split(matrix(stage, 8, level))
+            wh, wl = split(stage[64 * level : 64 * level + 64, :])
             vh, vl = split(current[:, :HALF])
             two = mm(jnp.concatenate([vh, vl], axis=0), wh)
             current = two[:16] + two[16:] + mm(vh, wl)
@@ -236,17 +236,19 @@
     copies[2].wait()
     lane_ids = lax.broadcasted_iota(jnp.int32, (1, 128), 1)
 
-    def pair_group(g, _):
+    def pair_layout(g, to):
         first = pl.multiple_of(32 * g, 16)
         second = pl.multiple_of(32 * g + 16, 16)
         paired(
-            stage,
+            to,
             16,
             lambda j: pairs[pl.ds(first, 16), lanes(j)].astype(f32),
             lambda j: pairs[pl.ds(second, 16), lanes(j)].astype(f32),
         )
+
+    def pair_products(g, at):
         for i in range(16):
-            weight = matrix(stage, 16, i).astype(bf16)
+            weight = matrix(at, 16, i).astype(bf16)
             listed = [32 * g + i, 32 * g + 16 + i]
             stacked = jnp.concatenate(
                 [table[src_ref[listed[0]]] * low16, table[src_ref[listed[1]]] * high16], axis=0
@@ -263,9 +265,18 @@
                 rows_at[pl.ds(owner * SLOTS + rank, 1), :] = jnp.where(
                     lane_ids == dst_ref[listed[k]], 1.0, 0.0
                 )
-        return 0
-
-    lax.fori_loop(0, PAIR_ROWS // 32, pair_group, 0)
+
+    groups = PAIR_ROWS // 32
+    pair_layout(0, stage)
+
+    def pair_step(h, _):
+        pair_layout(2 * h + 1, stage_two)
+        pair_products(2 * h, stage)
+        pair_layout(jnp.minimum(2 * h + 2, groups - 1), stage)
+        pair_products(2 * h + 1, stage_two)
+        return 0
+
+    lax.fori_loop(0, groups // 2, pair_step, 0)
 
     def place_rows(o, _):
         out_ref[o * TILES + SLOTS + 1] = rows_at[
@@ -278,7 +289,7 @@
 
 
 def mid_kernel(
-    after_ref, xs_ref, xe_ref, near_hbm, basis_hbm, edges_hbm, top_ref,
+    after_ref, xs_ref, xe_ref, near_hbm, basis_hbm, edges_hbm, top_ref, couple_ref,
     near_ref, down_ref, basis_ref, top_out_ref,
     near, basis, edges, stage, stage_two, vec_a, vec_b, highs, lows, sems,
 ):
@@ -291,7 +302,6 @@
         copy.start()
     low16, _ = half_masks(16)
     low64, high64 = half_masks(64)
-    flow = low_lanes(128)
 
     copies[0].wait()
 
@@ -326,6 +336,7 @@
     lax.fori_loop(0, 8, near_group, 0)
 
     copies[1].wait()
+    wide = low_lanes(64)
     even = (lax.broadcasted_iota(jnp.int32, (16, 128), 0) % 2) == 0
 
     def basis_group(g, _):
@@ -335,10 +346,11 @@
             turned = swap(tile)
             stage[pl.ds(32 * j, 16), :] = jnp.where(even, tile, turned)
             stage[pl.ds(32 * j + 16, 16), :] = jnp.where(even, turned, tile)
-        for i in range(16):
-            at = pl.multiple_of(g * 1024 + i * 64, 64)
-            value = matrix(stage, 16, i).astype(bf16)
-            basis_ref[pl.ds(at, 64), :] = value * (high64 if i % 2 else low64)
+        for i in range(0, 16, 2):
+            at = pl.multiple_of(g * 512 + i * 32, 64)
+            basis_ref[pl.ds(at, 64), :] = jnp.where(
+                wide, matrix(stage, 16, i), matrix(stage, 16, i + 1)
+            ).astype(bf16)
         return 0
 
     lax.fori_loop(0, 8, basis_group, 0)
@@ -362,12 +374,8 @@
                 there[2 * q] = found[:64]
                 there[2 * q + 1] = found[64:]
             else:
-                high = found.astype(bf16).astype(f32)
-                rest = found - high
                 at = pl.multiple_of(q * 128, 128)
-                down_ref[pl.ds(at, 128), :] = jnp.where(flow, high, swap(rest)).astype(bf16)
-                at = pl.multiple_of(q * 128 + FLAT, 128)
-                down_ref[pl.ds(at, 128), :] = jnp.where(flow, swap(high), rest).astype(bf16)
+                down_ref[pl.ds(at, 128), :] = found.astype(bf16)
 
         quarter = nodes // 4
         if quarter > 4:
@@ -384,11 +392,16 @@
         here, there = there, here
         nodes *= 2
 
-    paired(stage, 8, lambda j: top_ref[0:8, lanes(j)], lambda j: top_ref[8:16, lanes(j)])
     low = low_lanes(64)
+    low32 = low_lanes(32)
+    for level in range(LEVELS):
+        second = couple_ref[32 * level : 32 * level + 32, :]
+        first = top_ref[32 * level : 32 * level + 32, :] if level < LEVELS - 1 else second
+        stage[pl.ds(64 * level, 32, stride=2), :] = jnp.where(low32, first, swap(second))
+        stage[pl.ds(64 * level + 1, 32, stride=2), :] = jnp.where(low32, swap(first), second)
     chain = None
     for level in range(LEVELS):
-        value = matrix(stage, 8, level)
+        value = stage[64 * level : 64 * level + 64, :]
         if chain is None:
             found = value
         else:
@@ -401,46 +414,54 @@
 
 
 def down_kernel(
-    me_ref, got_ref, near_ref, down_ref, basis_ref, top_ref,
+    me_ref, got_hbm, near_hbm, down_hbm, basis_hbm, top_ref,
     out_ref,
-    values, target, far,
+    got, near, down, basis, values, target, far, hats, sems,
 ):
+    copies = [
+        pltpu.make_async_copy(got_hbm, got, sems.at[0]),
+        pltpu.make_async_copy(down_hbm, down, sems.at[1]),
+        pltpu.make_async_copy(basis_hbm, basis, sems.at[2]),
+        pltpu.make_async_copy(near_hbm, near, sems.at[3]),
+    ]
+    for copy in copies:
+        copy.start()
     low8 = low_lanes(8)
-    low16, _ = half_masks(16)
+    low16, high16 = half_masks(16)
+    copies[0].wait()
 
     def unpack(o, _):
         for s in range(SLOTS):
             at = pl.multiple_of((o * SLOTS + s) * 8, 8)
-            values[pl.ds(at, 8), :] = got_ref[o * TILES + s].astype(f32)
+            values[pl.ds(at, 8), :] = got[o * TILES + s].astype(f32)
         at = pl.multiple_of(o * SLOTS, 8)
-        target[pl.ds(at, 8), :] = got_ref[o * TILES + SLOTS + 1].astype(f32)
+        target[pl.ds(at, 8), :] = got[o * TILES + SLOTS + 1].astype(f32)
         return 0
 
     lax.fori_loop(0, PEERS, unpack, 0, unroll=4)
     landing = jnp.concatenate(
         [target[128 * i : 128 * i + 128, :].T for i in range(SLOTS)], axis=1
     ).astype(bf16)
-    for u in range(8):
-        chosen = values[pl.ds(u, PEERS * SLOTS, stride=8), :].astype(bf16)
-        far[128 * u : 128 * u + 128, :] = mm(landing, chosen)
+    for u in range(0, 8, 2):
+        chosen = jnp.concatenate(
+            [values[pl.ds(u + k, PEERS * SLOTS, stride=8), :] for k in range(2)], axis=1
+        ).astype(bf16)
+        found = mm(landing, chosen)
+        far[128 * u : 128 * u + 128, :] = found[:, :128]
+        far[128 * u + 128 : 128 * u + 256, :] = found[:, 128:]
 
     def doubled(tile):
         turned = swap(tile)
-        both = jnp.concatenate(
+        return jnp.concatenate(
             [jnp.where(low8, tile, turned), jnp.where(low8, turned, tile)], axis=0
         )
-        return both
-
-    def halves(value):
-        high, rest = split(value)
-        return jnp.concatenate([high, rest * low16], axis=0)
 
     me = me_ref[0]
     total = jnp.zeros((2 * NV, HALF), f32)
     for level in range(LEVELS):
         parts = []
         for x in range(2**level, 2 ** (level + 1)):
-            tile = got_ref[lax.bitwise_xor(me, x) * TILES + SLOTS].astype(f32)
+            tile = got[lax.bitwise_xor(me, x) * TILES + SLOTS].astype(f32)
             if len(parts) < 4:
                 parts.append(tile)
             else:
@@ -448,26 +469,45 @@
         tile = parts[0]
         for part in parts[1:]:
             tile = tile + part
-        total = total + mmt(halves(doubled(tile)), top_ref[level])
+        high, rest = split(doubled(tile))
+        total = total + mmt(jnp.concatenate([high, rest * low16], axis=0), top_ref[level])
     root = total[:NV] + total[NV:]
-    root = halves(jnp.concatenate([root, root], axis=1))
-
-    def leaf_pair(i):
-        at = pl.multiple_of(i * 128, 128)
-        two = mmt(root, down_ref[pl.ds(at, 128), :])
-        f0 = far[pl.ds(2 * i, 8, stride=128), :]
-        f1 = far[pl.ds(2 * i + 1, 8, stride=128), :]
-        gathered = jnp.concatenate(
-            [jnp.where(low8, f0, swap(f1)), jnp.where(low8, swap(f0), f1)], axis=0
-        )
-        hat = (two[:NV] + two[NV:] + gathered).astype(bf16)
-        out_ref[:, pl.ds(at, 128)] = mmt(hat, basis_ref[pl.ds(at, 128), :]) + near_ref[
-            :, pl.ds(at, 128)
-        ]
+    high, rest = split(jnp.concatenate([root, root], axis=1))
+    root = jnp.concatenate([high * low16, high * high16, rest * low16, rest * high16], axis=0)
+
+    copies[1].wait()
+
+    def hat_block(c, _):
+        at = pl.multiple_of(c * 512, 512)
+        found = mmt(root, down[pl.ds(at, 512), :])
+        for half in range(2):
+            block = found[16 * half : 16 * half + 16] + found[32 + 16 * half : 48 + 16 * half]
+            for k in range(4):
+                leaf = 64 * half + 8 * c + 2 * k
+                f0 = far[pl.ds(leaf, 8, stride=128), :]
+                f1 = far[pl.ds(leaf + 1, 8, stride=128), :]
+                gathered = jnp.concatenate(
+                    [jnp.where(low8, f0, swap(f1)), jnp.where(low8, swap(f0), f1)], axis=0
+                )
+                to = pl.multiple_of(half * FLAT + c * 512 + k * 128, 128)
+                hats[:, pl.ds(to, 128)] = (block[:, 128 * k : 128 * k + 128] + gathered).astype(
+                    bf16
+                )
+        return 0
+
+    lax.fori_loop(0, 8, hat_block, 0)
+    copies[2].wait()
+    copies[3].wait()
 
     def leaf_block(i, _):
         for k in range(8):
-            leaf_pair(8 * i + k)
+            at = pl.multiple_of(i * 1024 + k * 128, 128)
+            hat = hats[:, pl.ds(at, 128)]
+            weight = basis[pl.ds(pl.multiple_of(i * 512 + k * 64, 64), 64), :]
+            found = mmt(jnp.concatenate([hat * low16, hat * high16], axis=0), weight)
+            out_ref[:, pl.ds(at, 128)] = (
+                jnp.concatenate([found[:NV], found[NV:]], axis=1) + near[:, pl.ds(at, 128)]
+            )
         return 0
 
     lax.fori_loop(0, 8, leaf_block, 0)
@@ -485,8 +525,8 @@
     return pl.BlockSpec(memory_space=pl.ANY)
 
 
-def params():
-    return pltpu.CompilerParams(vmem_limit_bytes=VMEM_LIMIT)
+def params(mib):
+    return pltpu.CompilerParams(vmem_limit_bytes=mib * MIB)
 
 
 def shape(dims, dtype):
@@ -505,6 +545,7 @@
             pltpu.VMEM((EDGE_ROWS, FLAT), f32),
             pltpu.VMEM((PAIR_ROWS, FLAT), bf16),
             pltpu.VMEM((1024, 128), f32),
+            pltpu.VMEM((1024, 128), f32),
             pltpu.VMEM((64, NV, 128), f32),
             pltpu.VMEM((64, NV, 128), f32),
             pltpu.VMEM((128, 64, 128), bf16),
@@ -514,24 +555,24 @@
             pltpu.SMEM((PEERS,), jnp.int32),
             pltpu.SemaphoreType.DMA((3,)),
         ],
-        compiler_params=params(),
+        compiler_params=params(60),
         cost_estimate=pl.CostEstimate(
             flops=10**9, bytes_accessed=12 * 10**6, transcendentals=0
         ),
     )(me, src, own, dst, x_vecs, basis, edges, top_edges, pairs)
 
 
-def run_mid(after, xs, xe, near, basis, edges, top):
+def run_mid(after, xs, xe, near, basis, edges, top, couple):
     return pl.pallas_call(
         mid_kernel,
         name="mid",
         out_shape=(
             shape((NV, LEAF_DEV * LEAF), f32),
-            shape((LEAF_DEV * RANK, 128), bf16),
-            shape((LEAF_DEV * LEAF, 128), bf16),
+            shape((LEAF_DEV * RANK // 2, 128), bf16),
+            shape((LEAF_DEV * LEAF // 2, 128), bf16),
             shape((LEVELS, RANK, 128), bf16),
         ),
-        in_specs=[vmem(), vmem(), vmem(), hbm(), hbm(), hbm(), vmem()],
+        in_specs=[vmem(), vmem(), vmem(), hbm(), hbm(), hbm(), vmem(), vmem()],
         out_specs=(vmem(), vmem(), vmem(), vmem()),
         scratch_shapes=[
             pltpu.VMEM((LEAF_DEV, 3 * FLAT), bf16),
@@ -545,11 +586,11 @@
             pltpu.VMEM((128, 64, 128), bf16),
             pltpu.SemaphoreType.DMA((3,)),
         ],
-        compiler_params=params(),
+        compiler_params=params(24),
         cost_estimate=pl.CostEstimate(
             flops=10**9, bytes_accessed=14 * 10**6, transcendentals=0
         ),
-    )(after, xs, xe, near, basis, edges, top)
+    )(after, xs, xe, near, basis, edges, top, couple)
 
 
 def run_down(me, got, near, down, basis, top):
@@ -557,14 +598,20 @@
         down_kernel,
         name="down",
         out_shape=shape((NV, LEAF_DEV * LEAF), f32),
-        in_specs=[smem(), vmem(), vmem(), vmem(), vmem(), vmem()],
+        in_specs=[smem(), hbm(), hbm(), hbm(), hbm(), vmem()],
         out_specs=vmem(),
         scratch_shapes=[
+            pltpu.VMEM((PEERS * TILES, 8, 128), bf16),
+            pltpu.VMEM((NV, LEAF_DEV * LEAF), f32),
+            pltpu.VMEM((LEAF_DEV * RANK // 2, 128), bf16),
+            pltpu.VMEM((LEAF_DEV * LEAF // 2, 128), bf16),
             pltpu.VMEM((PEERS * SLOTS * 8, 128), f32),
             pltpu.VMEM((PEERS * SLOTS, 128), f32),
             pltpu.VMEM((8 * LEAF_DEV, 128), f32),
+            pltpu.VMEM((NV, LEAF_DEV * LEAF), bf16),
+            pltpu.SemaphoreType.DMA((4,)),
         ],
-        compiler_params=params(),
+        compiler_params=params(16),
         cost_estimate=pl.CostEstimate(
             flops=10**9, bytes_accessed=8 * 10**6, transcendentals=0
         ),
@@ -587,21 +634,22 @@
     back = [(target, source) for source, target in ahead]
     before = lax.ppermute(x_vecs[:, -LEAF:], "leaf", ahead)
     following = lax.ppermute(x_vecs[:, :LEAF], "leaf", back)
+    top_flat = top_edges.reshape((LEVELS - 1) * 32, 128)
     me = lax.axis_index("leaf").astype(jnp.int32).reshape(1)
     outgoing, after = run_up(
         me, couple_src, couple_owner.reshape(PAIR_ROWS), couple_dst, x_vecs, leaf_basis,
-        local_edges, top_edges[0], couple_blocks,
+        local_edges, top_flat, couple_blocks,
     )
+    outgoing, before, following = lax.optimization_barrier((outgoing, before, following))
     got = lax.all_to_all(
         outgoing.reshape(PEERS, TILES * 8, 128), "leaf", split_axis=0, concat_axis=0, tiled=True
     ).reshape(PEERS * TILES, 8, 128)
     fill = jnp.zeros((NV, LEAF), bf16)
     xs = jnp.concatenate([before, x_vecs, following], axis=1)
     xe = jnp.concatenate([x_vecs, following, fill], axis=1)
-    row = jnp.zeros((1, FLAT), f32)
-    top = jnp.concatenate([top_edges[0], row, row, top_couple[0], row], axis=0)
     near, down, basis, tops = run_mid(
-        after, xs, xe, near_blocks, leaf_basis, local_edges, top
+        after, xs, xe, near_blocks, leaf_basis, local_edges, top_flat,
+        top_couple.reshape(LEVELS * 32, 128),
     )
     return run_down(me, got, near, down, basis, tops)
 

time: 102 us -> 83.5 us (0.82)
  waiting for transfers between devices: 27.1 us -> 11.1 us
  Pallas kernels: 50.5 us -> 40.6 us
  local copies, waits for them, and re-layouts: 5.17 us -> 13.6 us
    ppermute x1, waiting for transfers between devices: 17.2 us -> 0.01 us  [shards(): following = lax.ppermute(x_vecs[:, :LEAF], 'leaf', back)]
    all_to_all x1, waiting for transfers between devices: 0.01 us -> 11.1 us  [shards(): lax.all_to_all(outgoing.reshape(PEERS, TILES * 8, 128), 'leaf', split_axi...]
    ppermute x1, waiting for transfers between devices: 9.92 us -> 0.01 us  [shards(): before = lax.ppermute(x_vecs[:, -LEAF:], 'leaf', ahead)]
    unnamed x10 -> x26, local copies, waits for them, and re-layouts: 3.22 us -> 11.5 us
    pallas_call x1, Pallas kernels: 20.4 us -> 15.7 us  [run_mid(): pl.pallas_call(mid_kernel, name='mid', out_shape=(shape((NV, LEAF_DEV * L...]
    pallas_call x1, Pallas kernels: 9.73 us -> 6.17 us  [run_down(): pl.pallas_call(down_kernel, name='down', out_shape=shape((NV, LEAF_DEV *...]
    all_to_all x1, starting transfers between devices: 11.2 us -> 9.11 us  [shards(): lax.all_to_all(outgoing.reshape(PEERS, TILES * 8, 128), 'leaf', split_axi...]
    pallas_call x1, Pallas kernels: 20.4 us -> 18.7 us  [run_up(): pl.pallas_call(up_kernel, name='up', out_shape=(shape((PEERS * TILES, 8,...]
  transfers between devices with their start and end apart: 3 -> 3, of which waited for: 2 -> 1; matrix products, arithmetic and copies ran while one was open for 3% -> 2% of each run, Pallas kernels for 20% -> 42%
where the time goes in v1:
time: 83.5 us; the launch traced here: 82.8 us
  Pallas kernels  40.6 us (49%)
  starting transfers between devices  17.3 us (21%)
  local copies, waits for them, and re-layouts  13.6 us (16%)
  waiting for transfers between devices  11.1 us (13%)
    pallas_call x1, Pallas kernels, run_up(): pl.pallas_call(up_kernel, name='up', out_shape=(shape((PEERS * TILES, 8,...  18.7 us
    pallas_call x1, Pallas kernels, run_mid(): pl.pallas_call(mid_kernel, name='mid', out_shape=(shape((NV, LEAF_DEV * L...  15.7 us
    unnamed x26, local copies, waits for them, and re-layouts  11.5 us
    all_to_all x1, waiting for transfers between devices, shards(): lax.all_to_all(outgoing.reshape(PEERS, TILES * 8, 128), 'leaf', split_axi...  11.1 us
    all_to_all x1, starting transfers between devices, shards(): lax.all_to_all(outgoing.reshape(PEERS, TILES * 8, 128), 'leaf', split_axi...  9.11 us
    ppermute x1, starting transfers between devices, shards(): following = lax.ppermute(x_vecs[:, :LEAF], 'leaf', back)  8.21 us
    pallas_call x1, Pallas kernels, run_down(): pl.pallas_call(down_kernel, name='down', out_shape=shape((NV, LEAF_DEV *...  6.17 us
  transfers between devices with their start and end apart: 3, of which 1 were waited for; matrix products, arithmetic and copies ran while one was open for 2% of the time, Pallas kernels for 42%

profile of v1, /device:TPU:0, one launch (start us, length us, event | category | flops | bytes accessed | tf_op | source)
XLA Modules:
  0.0 82.8 jit_solution(13920874193151640407)
XLA Ops:
  0.0 0.8 fusion
  0.8 8.2 %collective-permute-start.1 = (bf16[16,64]{1,0:T(8,128)(2,1)S(1)}, bf16[16,64]{1,0:T(8,128)(2,1)S(1)}, u32[]{:S(2)}, u32[]{:S(2)}) collective-permute-start(bf16[16,64]{1,0:T(8,128)(2,1)S(1)} %get-tuple-element.23), channel_id=1, source_target_pairs={{1,0},{2,1},{3,2},{4,3},{5,4},{6,5},{7,6},{8,7},{9,8},{10,9},{11,1... | collective-permute-start | bytes 6152 | tf_op jit(solution)/shard_map/ppermute | solution.py:636
  9.0 0.0 collective-permute-start
  9.0 18.7 %up.1 = (bf16[1280,8,128]{2,1,0:T(8,128)(2,1)}, f32[8,128]{1,0:T(8,128)}) custom-call(s32[1]{0:T(128)} %bitcast.me_ref, s32[512]{0:T(512)} %src_ref.1, s32[512]{0:T(512)} %bitcast.11, s32[512]{0:T(512)} %dst_ref.1, bf16[16,8192]{1,0:T(8,128)(2,1)} %x_ref.1, bf16[128,4096]{1,0:T(8,128)(2,1)} %basis_hbm.3, f32[254,4096]{1,0:T(8,128)} %edges_hbm.3, ...), custom_call_target="tpu_custom_call" | custom-call | flops 1000000000 | bytes 12000000 | tf_op jit(solution)/shard_map/up/pallas_call | solution.py:537
  27.7 0.0 copy-start.12
  27.7 0.0 copy-start.9
  27.7 0.0 copy-start.10
  27.8 0.0 copy-start.11
  27.8 9.1 %all-to-all-start = ((bf16[128,80,128]{2,1,0:T(8,128)(2,1)}), bf16[128,80,128]{2,1,0:T(8,128)(2,1)S(1)}, u32[]{:S(2)}, u32[]{:S(2)}) async-start(bf16[128,80,128]{2,1,0:T(8,128)(2,1)} %bitcast.10), calls=%async_computation | async-start | bytes 5242880 | tf_op jit(solution)/shard_map/all_to_all | solution.py:644
  36.9 0.1 concatenate.7.xe_ref
  37.0 1.2 %concatenate.6.xs_ref = bf16[16,8320]{1,0:T(8,128)(2,1)S(1)} concatenate(bf16[16,64]{1,0:T(8,128)(2,1)S(1)} %collective-permute-done, bf16[16,8192]{1,0:T(8,128)(2,1)} %x_ref.1, bf16[16,64]{1,0:T(8,128)(2,1)S(1)} %collective-permute-done.1), dimensions={1} | concatenate | bytes 532480 | tf_op jit(solution)/shard_map/concatenate | solution.py:648
  38.2 0.0 copy-start
  38.2 2.2 %copy-done = f32[254,4096]{1,0:T(8,128)S(1)} copy-done((f32[254,4096]{1,0:T(8,128)S(1)}, f32[254,4096]{1,0:T(8,128)}, u32[]{:S(2)}) %copy-start) | copy-done | bytes 4161560
  40.4 1.2 %copy-done.1 = bf16[128,4096]{1,0:T(8,128)(2,1)S(1)} copy-done((bf16[128,4096]{1,0:T(8,128)(2,1)S(1)}, bf16[128,4096]{1,0:T(8,128)(2,1)}, u32[]{:S(2)}) %copy-start.1) | copy-done | bytes 1048600
  41.7 1.9 %copy-done.2 = bf16[128,12288]{1,0:T(8,128)(2,1)S(1)} copy-done((bf16[128,12288]{1,0:T(8,128)(2,1)S(1)}, bf16[128,12288]{1,0:T(8,128)(2,1)}, u32[]{:S(2)}) %copy-start.2) | copy-done | bytes 3145752
  43.5 15.7 %mid.1 = (f32[16,8192]{1,0:T(8,128)S(1)}, bf16[4096,128]{1,0:T(8,128)(2,1)S(1)}, bf16[4096,128]{1,0:T(8,128)(2,1)S(1)}, bf16[7,64,128]{2,1,0:T(8,128)(2,1)S(1)}) custom-call(f32[8,128]{1,0:T(8,128)S(1)} %copy-done.11, bf16[16,8320]{1,0:T(8,128)(2,1)S(1)} %concatenate.6.xs_ref, bf16[16,8320]{1,0:T(8,128)(2,1)S(1)} %concatenate.7.xe_ref, ...), custom_call_target="tpu_custom_call" | custom-call | flops 1000000000 | bytes 14000000 | tf_op jit(solution)/shard_map/mid/pallas_call | solution.py:566
  59.3 0.9 %copy-done.3 = bf16[4096,128]{1,0:T(8,128)(2,1)} copy-done((bf16[4096,128]{1,0:T(8,128)(2,1)}, bf16[4096,128]{1,0:T(8,128)(2,1)S(1)}, u32[]{:S(2)}) %copy-start.3) | copy-done | bytes 1048600
  60.2 1.0 %copy-done.5 = bf16[4096,128]{1,0:T(8,128)(2,1)} copy-done((bf16[4096,128]{1,0:T(8,128)(2,1)}, bf16[4096,128]{1,0:T(8,128)(2,1)S(1)}, u32[]{:S(2)}) %copy-start.5) | copy-done | bytes 1048600
  61.2 0.8 copy-done.7
  62.0 11.1 %all-to-all-done = bf16[128,80,128]{2,1,0:T(8,128)(2,1)S(1)} async-done(((bf16[128,80,128]{2,1,0:T(8,128)(2,1)}), bf16[128,80,128]{2,1,0:T(8,128)(2,1)S(1)}, u32[]{:S(2)}, u32[]{:S(2)}) %all-to-all-start) | async-done | bytes 2621472 | tf_op jit(solution)/shard_map/all_to_all | solution.py:644
  73.1 1.2 %copy-done.4 = bf16[4096,128]{1,0:T(8,128)(2,1)S(1)} copy-done((bf16[4096,128]{1,0:T(8,128)(2,1)S(1)}, bf16[4096,128]{1,0:T(8,128)(2,1)}, u32[]{:S(2)}) %copy-start.4) | copy-done | bytes 1048600
  74.3 1.2 %copy-done.6 = bf16[4096,128]{1,0:T(8,128)(2,1)S(1)} copy-done((bf16[4096,128]{1,0:T(8,128)(2,1)S(1)}, bf16[4096,128]{1,0:T(8,128)(2,1)}, u32[]{:S(2)}) %copy-start.6) | copy-done | bytes 1048600
  75.6 1.0 %copy-done.8 = f32[16,8192]{1,0:T(8,128)S(1)} copy-done((f32[16,8192]{1,0:T(8,128)S(1)}, f32[16,8192]{1,0:T(8,128)}, u32[]{:S(2)}) %copy-start.8) | copy-done | bytes 524312
  76.6 6.2 %down.1 = f32[16,8192]{1,0:T(8,128)} custom-call(s32[1]{0:T(128)} %bitcast.me_ref, bf16[1280,8,128]{2,1,0:T(8,128)(2,1)S(1)} %bitcast.6, f32[16,8192]{1,0:T(8,128)S(1)} %copy-done.8, bf16[4096,128]{1,0:T(8,128)(2,1)S(1)} %copy-done.4, bf16[4096,128]{1,0:T(8,128)(2,1)S(1)} %copy-done.6, bf16[7,64,128]{2,1,0:T(8,128)(2,1)S(1)} %get-tuple-element.22.top_ref), custom_call_target="tpu_custom_call" | custom-call | flops 1000000000 | bytes 8000000 | tf_op jit(solution)/shard_map/down/pallas_call | solution.py:597
  (15 shorter events, 0.0 us)
Async XLA Ops:
  0.8 26.9 %collective-permute-start.1 = (bf16[16,64]{1,0:T(8,128)(2,1)S(1)}, bf16[16,64]{1,0:T(8,128)(2,1)S(1)}, u32[]{:S(2)}, u32[]{:S(2)}) collective-permute-start(bf16[16,64]{1,0:T(8,128)(2,1)S(1)} %get-tuple-element.23), channel_id=1, source_target_pairs={{1,0},{2,1},{3,2},{4,3},{5,4},{6,5},{7,6},{8,7},{9,8},{10,9},{11,1... | collective-permute-start | bytes 6152 | tf_op jit(solution)/shard_map/ppermute | solution.py:636
  9.0 18.7 %collective-permute-start = (bf16[16,64]{1,0:T(8,128)(2,1)S(1)}, bf16[16,64]{1,0:T(8,128)(2,1)S(1)}, u32[]{:S(2)}, u32[]{:S(2)}) collective-permute-start(bf16[16,64]{1,0:T(8,128)(2,1)S(1)} %get-tuple-element.24), channel_id=1, source_target_pairs={{0,1},{1,2},{2,3},{3,4},{4,5},{5,6},{6,7},{7,8},{8,9},{9,10},{10,1... | collective-permute-start | bytes 6152 | tf_op jit(solution)/shard_map/ppermute | solution.py:635
  27.7 9.2 %copy-start.12 = (bf16[16,8192]{1,0:T(8,128)(2,1)S(1)}, bf16[16,8192]{1,0:T(8,128)(2,1)}, u32[]{:S(2)}) copy-start(bf16[16,8192]{1,0:T(8,128)(2,1)} %x_ref.1) | copy-start | bytes 786436
  27.7 10.5 %copy-start.9 = (f32[1,6,4096]{2,0,1:T(1,128)S(1)}, f32[1,6,4096]{2,0,1:T(1,128)}, u32[]{:S(2)}) copy-start(f32[1,6,4096]{2,0,1:T(1,128)} %param.14) | copy-start | bytes 294916
  27.7 10.5 %copy-start.10 = (f32[1,7,4096]{2,0,1:T(1,128)S(1)}, f32[1,7,4096]{2,0,1:T(1,128)}, u32[]{:S(2)}) copy-start(f32[1,7,4096]{2,0,1:T(1,128)} %param.15) | copy-start | bytes 344068
  27.8 10.5 %copy-start.11 = (f32[8,128]{1,0:T(8,128)S(1)}, f32[8,128]{1,0:T(8,128)}, u32[]{:S(2)}) copy-start(f32[8,128]{1,0:T(8,128)} %get-tuple-element.16.after_ref) | copy-start | bytes 12292
  27.8 45.3 %all-to-all-start = ((bf16[128,80,128]{2,1,0:T(8,128)(2,1)}), bf16[128,80,128]{2,1,0:T(8,128)(2,1)S(1)}, u32[]{:S(2)}, u32[]{:S(2)}) async-start(bf16[128,80,128]{2,1,0:T(8,128)(2,1)} %bitcast.10), calls=%async_computation | async-start | bytes 5242880 | tf_op jit(solution)/shard_map/all_to_all | solution.py:644
  38.2 2.2 %copy-start = (f32[254,4096]{1,0:T(8,128)S(1)}, f32[254,4096]{1,0:T(8,128)}, u32[]{:S(2)}) copy-start(f32[254,4096]{1,0:T(8,128)} %edges_hbm.3) | copy-start | bytes 12484612
  40.4 1.2 %copy-start.1 = (bf16[128,4096]{1,0:T(8,128)(2,1)S(1)}, bf16[128,4096]{1,0:T(8,128)(2,1)}, u32[]{:S(2)}) copy-start(bf16[128,4096]{1,0:T(8,128)(2,1)} %basis_hbm.3) | copy-start | bytes 3145732
  41.6 1.9 %copy-start.2 = (bf16[128,12288]{1,0:T(8,128)(2,1)S(1)}, bf16[128,12288]{1,0:T(8,128)(2,1)}, u32[]{:S(2)}) copy-start(bf16[128,12288]{1,0:T(8,128)(2,1)} %near_hbm.1) | copy-start | bytes 9437188
  59.3 1.0 %copy-start.3 = (bf16[4096,128]{1,0:T(8,128)(2,1)}, bf16[4096,128]{1,0:T(8,128)(2,1)S(1)}, u32[]{:S(2)}) copy-start(bf16[4096,128]{1,0:T(8,128)(2,1)S(1)} %get-tuple-element.20.down_hbm) | copy-start | bytes 3145732
  60.2 1.0 %copy-start.5 = (bf16[4096,128]{1,0:T(8,128)(2,1)}, bf16[4096,128]{1,0:T(8,128)(2,1)S(1)}, u32[]{:S(2)}) copy-start(bf16[4096,128]{1,0:T(8,128)(2,1)S(1)} %get-tuple-element.21.basis_hbm) | copy-start | bytes 3145732
  61.2 0.8 copy-start.7
  73.1 1.2 %copy-start.4 = (bf16[4096,128]{1,0:T(8,128)(2,1)S(1)}, bf16[4096,128]{1,0:T(8,128)(2,1)}, u32[]{:S(2)}) copy-start(bf16[4096,128]{1,0:T(8,128)(2,1)} %copy-done.3) | copy-start | bytes 3145732
  74.3 1.2 %copy-start.6 = (bf16[4096,128]{1,0:T(8,128)(2,1)S(1)}, bf16[4096,128]{1,0:T(8,128)(2,1)}, u32[]{:S(2)}) copy-start(bf16[4096,128]{1,0:T(8,128)(2,1)} %copy-done.5) | copy-start | bytes 3145732
  75.6 1.0 %copy-start.8 = (f32[16,8192]{1,0:T(8,128)S(1)}, f32[16,8192]{1,0:T(8,128)}, u32[]{:S(2)}) copy-start(f32[16,8192]{1,0:T(8,128)} %copy-done.7) | copy-start | bytes 1572868

commit v2 on v1

--- a/solution.py
+++ b/solution.py
@@ -72,13 +72,13 @@
     return pl.ds(start + j * 128, 128)
 
 
-def relayout_edges(edges, stage, highs, lows):
-    def keep(index, place):
-        high, low = split(matrix(stage, 8, index))
+def relayout_edges(edges, stage, stage_two, highs, lows):
+    def keep(at, index, place):
+        high, low = split(matrix(at, 8, index))
         highs[place] = high
         lows[place] = low
 
-    def group(g, _):
+    def layout(g, to):
         first = jnp.where(
             g < 8, 8 * g, jnp.where(g < 12, 64 + 8 * g, jnp.where(g < 14, 96 + 8 * g, 224))
         )
@@ -86,77 +86,98 @@
         first = pl.multiple_of(first, 8)
         second = pl.multiple_of(first + gap, 8)
         paired(
-            stage,
+            to,
             8,
             lambda j: edges[pl.ds(first, 8), lanes(j)],
             lambda j: edges[pl.ds(second, 8), lanes(j)],
         )
+
+    def step(h, _):
+        odd = jnp.minimum(2 * h + 1, 14)
+        layout(2 * h, stage)
+        layout(odd, stage_two)
         for i in range(8):
-            keep(i, 8 * g + i)
-        return 0
-
-    lax.fori_loop(0, 15, group, 0)
+            keep(stage, i, 16 * h + i)
+        for i in range(8):
+            keep(stage_two, i, 8 * odd + i)
+        return 0
+
+    lax.fori_loop(0, 8, step, 0)
     paired(
         stage,
         8,
         lambda j: edges[240:248, lanes(j)],
         lambda j: pltpu.roll(edges[240:248, lanes(j)], 4, 0),
     )
-    for i in range(4):
-        keep(i, 120 + i)
     rows = lax.broadcasted_iota(jnp.int32, (8, 128), 0)
 
     def last_second(j):
         tile = edges[246:254, lanes(j)]
         return jnp.where(rows < 6, pltpu.roll(tile, 6, 0), pltpu.roll(tile, 7, 0))
 
-    paired(stage, 8, lambda j: edges[246:254, lanes(j)], last_second)
-    keep(2, 124)
-    keep(3, 125)
-    keep(6, 126)
+    paired(stage_two, 8, lambda j: edges[246:254, lanes(j)], last_second)
+    for i in range(4):
+        keep(stage, i, 120 + i)
+    keep(stage_two, 2, 124)
+    keep(stage_two, 3, 125)
+    keep(stage_two, 6, 126)
 
 
 def up_kernel(
-    me_ref, src_ref, own_ref, dst_ref, x_ref, basis_hbm, edges_hbm, top_ref, pairs_hbm,
+    x_ref, top_ref, src_hbm, own_hbm, dst_hbm, basis_hbm, edges_hbm, pairs_hbm,
     out_ref, done_ref,
-    basis, edges, pairs, stage, stage_two, vec_a, vec_b, highs, lows, table, rows_at, count, sems,
+    src_ref, own_ref, dst_ref, basis, edges, pairs, stage, stage_two, tops, vec_a, vec_b,
+    highs, lows, table, rows_at, count, sems,
 ):
-    copies = [
-        pltpu.make_async_copy(basis_hbm, basis, sems.at[0]),
-        pltpu.make_async_copy(edges_hbm, edges, sems.at[1]),
-        pltpu.make_async_copy(pairs_hbm, pairs, sems.at[2]),
+    basis_copy = pltpu.make_async_copy(basis_hbm, basis, sems.at[0])
+    edges_copy = pltpu.make_async_copy(edges_hbm, edges, sems.at[1])
+    pairs_copy = pltpu.make_async_copy(pairs_hbm, pairs, sems.at[2])
+    lists = [
+        pltpu.make_async_copy(src_hbm, src_ref, sems.at[3]),
+        pltpu.make_async_copy(own_hbm, own_ref, sems.at[4]),
+        pltpu.make_async_copy(dst_hbm, dst_ref, sems.at[5]),
     ]
-    for copy in copies:
+    basis_copy.start()
+    edges_copy.start()
+    for copy in lists:
         copy.start()
     low16, high16 = half_masks(16)
     low = low_lanes(16)
 
     def clear(i, _):
-        out_ref[pl.ds(i * 16, 16)] = jnp.zeros((16, 8, 128), bf16)
-        return 0
-
-    lax.fori_loop(0, PEERS * TILES // 16, clear, 0)
+        out_ref[pl.ds(i * 32, 32)] = jnp.zeros((32, 8, 128), bf16)
+        return 0
+
+    lax.fori_loop(0, PEERS * TILES // 32, clear, 0)
     rows_at[...] = jnp.zeros_like(rows_at)
 
     def clear_count(i, _):
-        count[i] = 0
-        return 0
-
-    lax.fori_loop(0, PEERS, clear_count, 0)
-
-    copies[0].wait()
-
-    def leaf_group(g, _):
+        for k in range(16):
+            count[16 * i + k] = 0
+        return 0
+
+    lax.fori_loop(0, PEERS // 16, clear_count, 0)
+    for level in range(LEVELS - 1):
+        tile = top_ref[32 * level : 32 * level + 32, :]
+        tops[pl.ds(64 * level, 32, stride=2), :] = tile
+        tops[pl.ds(64 * level + 1, 32, stride=2), :] = swap(tile)
+
+    basis_copy.wait()
+    pairs_copy.start()
+
+    def leaf_layout(g, to):
         first = pl.multiple_of(16 * g, 16)
         second = pl.multiple_of(64 + 16 * g, 16)
         paired(
-            stage,
+            to,
             16,
             lambda j: basis[pl.ds(first, 16), lanes(j)].astype(f32),
             lambda j: basis[pl.ds(second, 16), lanes(j)].astype(f32),
         )
+
+    def leaf_products(g, at_stage):
         for i in range(0, 16, 2):
-            weight = jnp.concatenate([matrix(stage, 16, i), matrix(stage, 16, i + 1)], axis=0)
+            weight = jnp.concatenate([matrix(at_stage, 16, i), matrix(at_stage, 16, i + 1)], axis=0)
             at = pl.multiple_of(g * 1024 + i * 64, 128)
             left = x_ref[:, pl.ds(at, 128)]
             right = x_ref[:, pl.ds(pl.multiple_of(at + FLAT, 128), 128)]
@@ -171,19 +192,25 @@
                 vec_a[t] = pair
                 table[t] = jnp.where(low, pair, turned).astype(bf16)
                 table[t + 64] = jnp.where(low, turned, pair).astype(bf16)
-        return 0
-
-    lax.fori_loop(0, 4, leaf_group, 0)
-
-    copies[1].wait()
-    relayout_edges(edges, stage, highs, lows)
-
-    here, there = vec_a, vec_b
-    nodes = LEAF_DEV
-    while nodes > 2:
+
+    def leaf_step(h, _):
+        leaf_layout(2 * h, stage)
+        leaf_layout(2 * h + 1, stage_two)
+        leaf_products(2 * h, stage)
+        leaf_products(2 * h + 1, stage_two)
+        return 0
+
+    lax.fori_loop(0, 2, leaf_step, 0)
+
+    edges_copy.wait()
+    relayout_edges(edges, stage, stage_two, highs, lows)
+
+    def parents(nodes, first, amount):
+        up = nodes in (128, 32, 8)
+        here, there = (vec_a, vec_b) if up else (vec_b, vec_a)
         base = LEVEL_BASE[nodes]
-
-        def parent(q, here=here, there=there, base=base):
+        for k in range(amount):
+            q = first + k
             p0 = here[2 * q]
             p1 = here[2 * q + 1]
             both = jnp.concatenate(
@@ -196,44 +223,30 @@
             found = two[:32] + two[32:] + mm(vh, wl)
             there[q] = jnp.where(low, found[:16], found[16:])
 
-        quarter = nodes // 4
-        if quarter > 8:
-
-            def block(i, _, parent=parent):
-                for k in range(8):
-                    parent(8 * i + k)
-                return 0
-
-            lax.fori_loop(0, quarter // 8, block, 0)
-        else:
-            for q in range(quarter):
-                parent(q)
-        here, there = there, here
-        nodes //= 2
-    last = here[0]
-    both = jnp.concatenate([last, swap(last)], axis=0)[:, :HALF]
-    vh, vl = split(both)
-    wh = highs[126]
-    two = mm(jnp.concatenate([vh, vl], axis=0), wh)
-    found = two[:32] + two[32:] + mm(vh, lows[126])
-    current = found[:16] + swap(found[16:])
-
-    for level in range(LEVELS - 1):
-        tile = top_ref[32 * level : 32 * level + 32, :]
-        stage[pl.ds(64 * level, 32, stride=2), :] = tile
-        stage[pl.ds(64 * level + 1, 32, stride=2), :] = swap(tile)
-    me = me_ref[0]
-    for level in range(LEVELS):
+    def root():
+        last = vec_a[0]
+        both = jnp.concatenate([last, swap(last)], axis=0)[:, :HALF]
+        vh, vl = split(both)
+        two = mm(jnp.concatenate([vh, vl], axis=0), highs[126])
+        found = two[:32] + two[32:] + mm(vh, lows[126])
+        return found[:16] + swap(found[16:])
+
+    def carried(current, level):
+        wh, wl = split(tops[64 * level : 64 * level + 64, :])
+        vh, vl = split(current[:, :HALF])
+        two = mm(jnp.concatenate([vh, vl], axis=0), wh)
+        return two[:16] + two[16:] + mm(vh, wl)
+
+    me = lax.axis_index("leaf").astype(jnp.int32)
+
+    def send(current, level):
         tile = join(current[0:8], current[8:16]).astype(bf16)
         for x in range(2**level, 2 ** (level + 1)):
             out_ref[lax.bitwise_xor(me, x) * TILES + SLOTS] = tile
-        if level < LEVELS - 1:
-            wh, wl = split(stage[64 * level : 64 * level + 64, :])
-            vh, vl = split(current[:, :HALF])
-            two = mm(jnp.concatenate([vh, vl], axis=0), wh)
-            current = two[:16] + two[16:] + mm(vh, wl)
-
-    copies[2].wait()
+
+    for copy in lists:
+        copy.wait()
+    pairs_copy.wait()
     lane_ids = lax.broadcasted_iota(jnp.int32, (1, 128), 1)
 
     def pair_layout(g, to):
@@ -247,14 +260,24 @@
         )
 
     def pair_products(g, at):
-        for i in range(16):
-            weight = matrix(at, 16, i).astype(bf16)
-            listed = [32 * g + i, 32 * g + 16 + i]
+        zero = jnp.zeros((32, 128), bf16)
+        for i in range(0, 16, 2):
+            weight = jnp.concatenate(
+                [matrix(at, 16, i), matrix(at, 16, i + 1)], axis=1
+            ).astype(bf16)
+            listed = [32 * g + i, 32 * g + 16 + i, 32 * g + i + 1, 32 * g + 17 + i]
+            sources = [table[src_ref[r]] for r in listed]
+            first = jnp.concatenate([sources[0] * low16, sources[1] * high16], axis=0)
+            second = jnp.concatenate([sources[2] * low16, sources[3] * high16], axis=0)
             stacked = jnp.concatenate(
-                [table[src_ref[listed[0]]] * low16, table[src_ref[listed[1]]] * high16], axis=0
+                [
+                    jnp.concatenate([first, zero], axis=1),
+                    jnp.concatenate([zero, second], axis=1),
+                ],
+                axis=0,
             )
             found = mmt(stacked, weight)
-            for k in range(2):
+            for k in range(4):
                 owner = own_ref[listed[k]]
                 rank = count[owner]
                 count[owner] = rank + 1
@@ -269,14 +292,34 @@
     groups = PAIR_ROWS // 32
     pair_layout(0, stage)
 
-    def pair_step(h, _):
+    def pair_step(h):
         pair_layout(2 * h + 1, stage_two)
         pair_products(2 * h, stage)
         pair_layout(jnp.minimum(2 * h + 2, groups - 1), stage)
         pair_products(2 * h + 1, stage_two)
-        return 0
-
-    lax.fori_loop(0, groups // 2, pair_step, 0)
+
+    def first_steps(h, _):
+        parents(128, 8 * h, 8)
+        pair_step(h)
+        return 0
+
+    lax.fori_loop(0, 4, first_steps, 0)
+    parents(64, 0, 16)
+    pair_step(4)
+    parents(32, 0, 8)
+    parents(16, 0, 4)
+    pair_step(5)
+    parents(8, 0, 2)
+    parents(4, 0, 1)
+    current = root()
+    send(current, 0)
+    current = carried(current, 0)
+    pair_step(6)
+    for level in range(1, LEVELS):
+        send(current, level)
+        if level < LEVELS - 1:
+            current = carried(current, level)
+    pair_step(7)
 
     def place_rows(o, _):
         out_ref[o * TILES + SLOTS + 1] = rows_at[
@@ -284,7 +327,7 @@
         ].astype(bf16)
         return 0
 
-    lax.fori_loop(0, PEERS, place_rows, 0, unroll=8)
+    lax.fori_loop(0, PEERS, place_rows, 0, unroll=16)
     done_ref[...] = current[0:8]
 
 
@@ -356,7 +399,7 @@
     lax.fori_loop(0, 8, basis_group, 0)
 
     copies[2].wait()
-    relayout_edges(edges, stage, highs, lows)
+    relayout_edges(edges, stage, stage_two, highs, lows)
     vec_a[0] = highs[126].astype(f32) + lows[126].astype(f32)
     here, there = vec_a, vec_b
     nodes = 4
@@ -414,7 +457,7 @@
 
 
 def down_kernel(
-    me_ref, got_hbm, near_hbm, down_hbm, basis_hbm, top_ref,
+    got_hbm, near_hbm, down_hbm, basis_hbm, top_ref,
     out_ref,
     got, near, down, basis, values, target, far, hats, sems,
 ):
@@ -456,7 +499,7 @@
             [jnp.where(low8, tile, turned), jnp.where(low8, turned, tile)], axis=0
         )
 
-    me = me_ref[0]
+    me = lax.axis_index("leaf").astype(jnp.int32)
     total = jnp.zeros((2 * NV, HALF), f32)
     for level in range(LEVELS):
         parts = []
@@ -517,12 +560,8 @@
     return pl.BlockSpec(memory_space=pltpu.VMEM)
 
 
-def smem():
-    return pl.BlockSpec(memory_space=pltpu.SMEM)
-
-
 def hbm():
-    return pl.BlockSpec(memory_space=pl.ANY)
+    return pl.BlockSpec(memory_space=pltpu.HBM)
 
 
 def params(mib):
@@ -533,19 +572,23 @@
     return jax.ShapeDtypeStruct(dims, dtype)
 
 
-def run_up(me, src, own, dst, x_vecs, basis, edges, top_edges, pairs):
+def run_up(src, own, dst, x_vecs, basis, edges, top_edges, pairs):
     return pl.pallas_call(
         up_kernel,
         name="up",
         out_shape=(shape((PEERS * TILES, 8, 128), bf16), shape((8, 128), f32)),
-        in_specs=[smem(), smem(), smem(), smem(), vmem(), hbm(), hbm(), vmem(), hbm()],
+        in_specs=[vmem(), vmem(), hbm(), hbm(), hbm(), hbm(), hbm(), hbm()],
         out_specs=(vmem(), vmem()),
         scratch_shapes=[
+            pltpu.SMEM((PAIR_ROWS,), jnp.int32),
+            pltpu.SMEM((PAIR_ROWS,), jnp.int32),
+            pltpu.SMEM((PAIR_ROWS,), jnp.int32),
             pltpu.VMEM((LEAF_DEV, FLAT), bf16),
             pltpu.VMEM((EDGE_ROWS, FLAT), f32),
             pltpu.VMEM((PAIR_ROWS, FLAT), bf16),
             pltpu.VMEM((1024, 128), f32),
             pltpu.VMEM((1024, 128), f32),
+            pltpu.VMEM((64 * (LEVELS - 1), 128), f32),
             pltpu.VMEM((64, NV, 128), f32),
             pltpu.VMEM((64, NV, 128), f32),
             pltpu.VMEM((128, 64, 128), bf16),
@@ -553,13 +596,13 @@
             pltpu.VMEM((LEAF_DEV, NV, 128), bf16),
             pltpu.VMEM((PEERS * SLOTS, 128), f32),
             pltpu.SMEM((PEERS,), jnp.int32),
-            pltpu.SemaphoreType.DMA((3,)),
+            pltpu.SemaphoreType.DMA((6,)),
         ],
         compiler_params=params(60),
         cost_estimate=pl.CostEstimate(
             flops=10**9, bytes_accessed=12 * 10**6, transcendentals=0
         ),
-    )(me, src, own, dst, x_vecs, basis, edges, top_edges, pairs)
+    )(x_vecs, top_edges, src, own, dst, basis, edges, pairs)
 
 
 def run_mid(after, xs, xe, near, basis, edges, top, couple):
@@ -586,19 +629,25 @@
             pltpu.VMEM((128, 64, 128), bf16),
             pltpu.SemaphoreType.DMA((3,)),
         ],
-        compiler_params=params(24),
+        compiler_params=params(60),
         cost_estimate=pl.CostEstimate(
             flops=10**9, bytes_accessed=14 * 10**6, transcendentals=0
         ),
     )(after, xs, xe, near, basis, edges, top, couple)
 
 
-def run_down(me, got, near, down, basis, top):
+def run_down(got, near, down, basis, top):
     return pl.pallas_call(
         down_kernel,
         name="down",
         out_shape=shape((NV, LEAF_DEV * LEAF), f32),
-        in_specs=[smem(), hbm(), hbm(), hbm(), hbm(), vmem()],
+        in_specs=[
+            pl.BlockSpec(memory_space=pl.ANY),
+            hbm(),
+            hbm(),
+            hbm(),
+            vmem(),
+        ],
         out_specs=vmem(),
         scratch_shapes=[
             pltpu.VMEM((PEERS * TILES, 8, 128), bf16),
@@ -611,11 +660,11 @@
             pltpu.VMEM((NV, LEAF_DEV * LEAF), bf16),
             pltpu.SemaphoreType.DMA((4,)),
         ],
-        compiler_params=params(16),
+        compiler_params=params(59),
         cost_estimate=pl.CostEstimate(
             flops=10**9, bytes_accessed=8 * 10**6, transcendentals=0
         ),
-    )(me, got, near, down, basis, top)
+    )(got, near, down, basis, top)
 
 
 def shards(
@@ -635,9 +684,8 @@
     before = lax.ppermute(x_vecs[:, -LEAF:], "leaf", ahead)
     following = lax.ppermute(x_vecs[:, :LEAF], "leaf", back)
     top_flat = top_edges.reshape((LEVELS - 1) * 32, 128)
-    me = lax.axis_index("leaf").astype(jnp.int32).reshape(1)
     outgoing, after = run_up(
-        me, couple_src, couple_owner.reshape(PAIR_ROWS), couple_dst, x_vecs, leaf_basis,
+        couple_src, couple_owner.reshape(PAIR_ROWS), couple_dst, x_vecs, leaf_basis,
         local_edges, top_flat, couple_blocks,
     )
     outgoing, before, following = lax.optimization_barrier((outgoing, before, following))
@@ -651,7 +699,7 @@
         after, xs, xe, near_blocks, leaf_basis, local_edges, top_flat,
         top_couple.reshape(LEVELS * 32, 128),
     )
-    return run_down(me, got, near, down, basis, tops)
+    return run_down(got, near, down, basis, tops)
 
 
 def solution(mesh):

time: 83.5 us -> 80.3 us (0.962)
  local copies, waits for them, and re-layouts: 13.6 us -> 4.06 us
  waiting for transfers between devices: 11.1 us -> 16.3 us
  Pallas kernels: 40.6 us -> 42 us
    unnamed x26 -> x4, local copies, waits for them, and re-layouts: 11.5 us -> 1.52 us
    all_to_all x1, waiting for transfers between devices: 11.1 us -> 16.3 us  [shards(): lax.all_to_all(outgoing.reshape(PEERS, TILES * 8, 128), 'leaf', split_axi...]
    pallas_call x1, Pallas kernels: 18.7 us -> 15.4 us  [run_up(): pl.pallas_call(up_kernel, name='up', out_shape=(shape((PEERS * TILES, 8,...]
    pallas_call x1, Pallas kernels: 15.7 us -> 18.1 us  [run_mid(): pl.pallas_call(mid_kernel, name='mid', out_shape=(shape((NV, LEAF_DEV * L...]
    pallas_call x1, Pallas kernels: 6.17 us -> 8.44 us  [run_down(): pl.pallas_call(down_kernel, name='down', out_shape=shape((NV, LEAF_DEV *...]
where the time goes in v2:
time: 80.3 us; the launch traced here: 79.7 us
  Pallas kernels  42 us (52%)
  starting transfers between devices  17.3 us (22%)
  waiting for transfers between devices  16.3 us (20%)
  local copies, waits for them, and re-layouts  4.06 us (5%)
    pallas_call x1, Pallas kernels, run_mid(): pl.pallas_call(mid_kernel, name='mid', out_shape=(shape((NV, LEAF_DEV * L...  18.1 us
    all_to_all x1, waiting for transfers between devices, shards(): lax.all_to_all(outgoing.reshape(PEERS, TILES * 8, 128), 'leaf', split_axi...  16.3 us
    pallas_call x1, Pallas kernels, run_up(): pl.pallas_call(up_kernel, name='up', out_shape=(shape((PEERS * TILES, 8,...  15.4 us
    all_to_all x1, starting transfers between devices, shards(): lax.all_to_all(outgoing.reshape(PEERS, TILES * 8, 128), 'leaf', split_axi...  9.1 us
    pallas_call x1, Pallas kernels, run_down(): pl.pallas_call(down_kernel, name='down', out_shape=shape((NV, LEAF_DEV *...  8.44 us
    ppermute x1, starting transfers between devices, shards(): following = lax.ppermute(x_vecs[:, :LEAF], 'leaf', back)  8.21 us
  transfers between devices with their start and end apart: 3, of which 1 were waited for; matrix products, arithmetic and copies ran while one was open for 2% of the time, Pallas kernels for 42%

profile of v2, /device:TPU:0, one launch (start us, length us, event | category | flops | bytes accessed | tf_op | source)
XLA Modules:
  0.0 79.7 jit_solution(12620856971446469046)
XLA Ops:
  0.0 0.8 fusion
  0.8 8.2 %collective-permute-start.1 = (bf16[16,64]{1,0:T(8,128)(2,1)S(1)}, bf16[16,64]{1,0:T(8,128)(2,1)S(1)}, u32[]{:S(2)}, u32[]{:S(2)}) collective-permute-start(bf16[16,64]{1,0:T(8,128)(2,1)S(1)} %get-tuple-element.23), channel_id=1, source_target_pairs={{1,0},{2,1},{3,2},{4,3},{5,4},{6,5},{7,6},{8,7},{9,8},{10,9},{11,1... | collective-permute-start | bytes 6152 | tf_op jit(solution)/shard_map/ppermute | solution.py:685
  9.0 0.0 collective-permute-start
  9.0 15.4 %up.1 = (bf16[1280,8,128]{2,1,0:T(8,128)(2,1)}, f32[8,128]{1,0:T(8,128)}) custom-call(bf16[16,8192]{1,0:T(8,128)(2,1)} %x_ref.1, f32[192,128]{1,0:T(8,128)} %bitcast.7, s32[512]{0:T(512)} %src_hbm.1, s32[512]{0:T(512)} %bitcast.10, s32[512]{0:T(512)} %dst_hbm.1, bf16[128,4096]{1,0:T(8,128)(2,1)} %basis_hbm.3, f32[254,4096]{1,0:T(8,128)} %edges_hbm.3, ...), custom_call_target="tpu_custom_call" | custom-call | flops 1000000000 | bytes 12000000 | tf_op jit(solution)/shard_map/up/pallas_call | solution.py:576
  24.4 0.0 copy-start.1
  24.4 0.0 collective-permute-done.1
  24.4 0.0 collective-permute-done
  24.5 9.1 %all-to-all-start = ((bf16[128,80,128]{2,1,0:T(8,128)(2,1)}), bf16[128,80,128]{2,1,0:T(8,128)(2,1)S(1)}, u32[]{:S(2)}, u32[]{:S(2)}) async-start(bf16[128,80,128]{2,1,0:T(8,128)(2,1)} %bitcast.6), calls=%async_computation | async-start | bytes 5242880 | tf_op jit(solution)/shard_map/all_to_all | solution.py:692
  33.6 0.0 copy-done.1
  33.6 0.8 %concatenate.7.xe_ref = bf16[16,8320]{1,0:T(8,128)(2,1)} concatenate(bf16[16,8192]{1,0:T(8,128)(2,1)S(1)} %copy-done.1, bf16[16,64]{1,0:T(8,128)(2,1)S(1)} %collective-permute-done.1, bf16[16,64]{1,0:T(8,128)(2,1)S(1)} %broadcast_in_dim.3), dimensions={1} | concatenate | bytes 532480 | tf_op jit(solution)/shard_map/concatenate | solution.py:697
  34.4 0.9 %concatenate.6.xs_ref = bf16[16,8320]{1,0:T(8,128)(2,1)} concatenate(bf16[16,64]{1,0:T(8,128)(2,1)S(1)} %collective-permute-done, bf16[16,8192]{1,0:T(8,128)(2,1)S(1)} %copy-done.1, bf16[16,64]{1,0:T(8,128)(2,1)S(1)} %collective-permute-done.1), dimensions={1} | concatenate | bytes 532480 | tf_op jit(solution)/shard_map/concatenate | solution.py:696
  35.3 18.1 %mid.1 = (f32[16,8192]{1,0:T(8,128)}, bf16[4096,128]{1,0:T(8,128)(2,1)}, bf16[4096,128]{1,0:T(8,128)(2,1)}, bf16[7,64,128]{2,1,0:T(8,128)(2,1)}) custom-call(f32[8,128]{1,0:T(8,128)} %get-tuple-element.16.after_ref, bf16[16,8320]{1,0:T(8,128)(2,1)} %concatenate.6.xs_ref, bf16[16,8320]{1,0:T(8,128)(2,1)} %concatenate.7.xe_ref, bf16[128,12288]{1,0:T(8,128)(2,1)} %near_hbm.1, ...), custom_call_target="tpu_custom_call" | custom-call | flops 1000000000 | bytes 14000000 | tf_op jit(solution)/shard_map/mid/pallas_call | solution.py:609
  53.5 16.3 %all-to-all-done = bf16[128,80,128]{2,1,0:T(8,128)(2,1)S(1)} async-done(((bf16[128,80,128]{2,1,0:T(8,128)(2,1)}), bf16[128,80,128]{2,1,0:T(8,128)(2,1)S(1)}, u32[]{:S(2)}, u32[]{:S(2)}) %all-to-all-start) | async-done | bytes 2621472 | tf_op jit(solution)/shard_map/all_to_all | solution.py:692
  69.8 0.0 copy-start
  69.8 1.5 %copy-done = bf16[128,80,128]{2,1,0:T(8,128)(2,1)} copy-done((bf16[128,80,128]{2,1,0:T(8,128)(2,1)}, bf16[128,80,128]{2,1,0:T(8,128)(2,1)S(1)}, u32[]{:S(2)}) %copy-start) | copy-done | bytes 2621464
  71.3 8.4 %down.1 = f32[16,8192]{1,0:T(8,128)} custom-call(bf16[1280,8,128]{2,1,0:T(8,128)(2,1)} %bitcast.5, f32[16,8192]{1,0:T(8,128)} %get-tuple-element.19.near_hbm, bf16[4096,128]{1,0:T(8,128)(2,1)} %get-tuple-element.20.down_hbm, bf16[4096,128]{1,0:T(8,128)(2,1)} %get-tuple-element.21.basis_hbm, bf16[7,64,128]{2,1,0:T(8,128)(2,1)} %get-tuple-element.22.top_ref), custom_call_target="tpu_custom_call" | custom-call | flops 1000000000 | bytes 8000000 | tf_op jit(solution)/shard_map/down/pallas_call | solution.py:640
  (1 shorter events, 0.0 us)
Async XLA Ops:
  0.8 23.7 %collective-permute-start.1 = (bf16[16,64]{1,0:T(8,128)(2,1)S(1)}, bf16[16,64]{1,0:T(8,128)(2,1)S(1)}, u32[]{:S(2)}, u32[]{:S(2)}) collective-permute-start(bf16[16,64]{1,0:T(8,128)(2,1)S(1)} %get-tuple-element.23), channel_id=1, source_target_pairs={{1,0},{2,1},{3,2},{4,3},{5,4},{6,5},{7,6},{8,7},{9,8},{10,9},{11,1... | collective-permute-start | bytes 6152 | tf_op jit(solution)/shard_map/ppermute | solution.py:685
  9.0 15.5 %collective-permute-start = (bf16[16,64]{1,0:T(8,128)(2,1)S(1)}, bf16[16,64]{1,0:T(8,128)(2,1)S(1)}, u32[]{:S(2)}, u32[]{:S(2)}) collective-permute-start(bf16[16,64]{1,0:T(8,128)(2,1)S(1)} %get-tuple-element.24), channel_id=1, source_target_pairs={{0,1},{1,2},{2,3},{3,4},{4,5},{5,6},{6,7},{7,8},{8,9},{9,10},{10,1... | collective-permute-start | bytes 6152 | tf_op jit(solution)/shard_map/ppermute | solution.py:684
  24.4 9.2 %copy-start.1 = (bf16[16,8192]{1,0:T(8,128)(2,1)S(1)}, bf16[16,8192]{1,0:T(8,128)(2,1)}, u32[]{:S(2)}) copy-start(bf16[16,8192]{1,0:T(8,128)(2,1)} %x_ref.1) | copy-start | bytes 786436
  24.5 45.3 %all-to-all-start = ((bf16[128,80,128]{2,1,0:T(8,128)(2,1)}), bf16[128,80,128]{2,1,0:T(8,128)(2,1)S(1)}, u32[]{:S(2)}, u32[]{:S(2)}) async-start(bf16[128,80,128]{2,1,0:T(8,128)(2,1)} %bitcast.6), calls=%async_computation | async-start | bytes 5242880 | tf_op jit(solution)/shard_map/all_to_all | solution.py:692
  69.8 1.5 %copy-start = (bf16[128,80,128]{2,1,0:T(8,128)(2,1)}, bf16[128,80,128]{2,1,0:T(8,128)(2,1)S(1)}, u32[]{:S(2)}) copy-start(bf16[128,80,128]{2,1,0:T(8,128)(2,1)S(1)} %all-to-all-done) | copy-start | bytes 7864324

commit v3 on v2

--- a/solution.py
+++ b/solution.py
@@ -14,6 +14,7 @@
 SLOTS = 8
 TILES = SLOTS + 2
 PAIR_ROWS = 512
+CHUNKS = 4
 EDGE_ROWS = 254
 FLAT = 4096
 HALF = 64
@@ -333,7 +334,7 @@
 
 def mid_kernel(
     after_ref, xs_ref, xe_ref, near_hbm, basis_hbm, edges_hbm, top_ref, couple_ref,
-    near_ref, down_ref, basis_ref, top_out_ref,
+    near_ref, down_ref, basis_ref, top_out_ref, ends_ref,
     near, basis, edges, stage, stage_two, vec_a, vec_b, highs, lows, sems,
 ):
     copies = [
@@ -374,9 +375,15 @@
                 )
                 found.append(mmt(vec, weight))
             near_ref[:, pl.ds(at, 128)] = jnp.concatenate(found, axis=1)
+
+        @pl.when(g == 0)
+        def _():
+            vec_a[0] = matrix(stage, 16, 0)
+
         return 0
 
     lax.fori_loop(0, 8, near_group, 0)
+    ends_ref[...] = join(vec_a[0], matrix(stage_two, 16, 15)).astype(bf16)
 
     copies[1].wait()
     wide = low_lanes(64)
@@ -457,21 +464,28 @@
 
 
 def down_kernel(
-    got_hbm, near_hbm, down_hbm, basis_hbm, top_ref,
+    got_hbm, near_hbm, down_hbm, basis_hbm, top_ref, ends_ref, before_ref, following_ref,
     out_ref,
-    got, near, down, basis, values, target, far, hats, sems,
+    got, near, down, basis, values, target, far, sems,
 ):
+    span = PEERS // CHUNKS
+    arriving = [
+        pltpu.make_async_copy(
+            got_hbm.at[pl.ds(c * span * TILES, span * TILES)],
+            got.at[pl.ds(c * span * TILES, span * TILES)],
+            sems.at[c],
+        )
+        for c in range(CHUNKS)
+    ]
     copies = [
-        pltpu.make_async_copy(got_hbm, got, sems.at[0]),
-        pltpu.make_async_copy(down_hbm, down, sems.at[1]),
-        pltpu.make_async_copy(basis_hbm, basis, sems.at[2]),
-        pltpu.make_async_copy(near_hbm, near, sems.at[3]),
+        pltpu.make_async_copy(down_hbm, down, sems.at[CHUNKS]),
+        pltpu.make_async_copy(basis_hbm, basis, sems.at[CHUNKS + 1]),
+        pltpu.make_async_copy(near_hbm, near, sems.at[CHUNKS + 2]),
     ]
-    for copy in copies:
+    for copy in arriving:
         copy.start()
     low8 = low_lanes(8)
     low16, high16 = half_masks(16)
-    copies[0].wait()
 
     def unpack(o, _):
         for s in range(SLOTS):
@@ -481,7 +495,12 @@
         target[pl.ds(at, 8), :] = got[o * TILES + SLOTS + 1].astype(f32)
         return 0
 
-    lax.fori_loop(0, PEERS, unpack, 0, unroll=4)
+    for c in range(CHUNKS):
+        arriving[c].wait()
+        if c == CHUNKS - 2:
+            for copy in copies:
+                copy.start()
+        lax.fori_loop(c * span, (c + 1) * span, unpack, 0, unroll=4)
     landing = jnp.concatenate(
         [target[128 * i : 128 * i + 128, :].T for i in range(SLOTS)], axis=1
     ).astype(bf16)
@@ -518,13 +537,14 @@
     high, rest = split(jnp.concatenate([root, root], axis=1))
     root = jnp.concatenate([high * low16, high * high16, rest * low16, rest * high16], axis=0)
 
-    copies[1].wait()
-
-    def hat_block(c, _):
-        at = pl.multiple_of(c * 512, 512)
-        found = mmt(root, down[pl.ds(at, 512), :])
+    for copy in copies:
+        copy.wait()
+    zero = jnp.zeros((2 * NV, 128), bf16)
+    for c in range(8):
+        found = mmt(root, down[512 * c : 512 * c + 512, :])
         for half in range(2):
             block = found[16 * half : 16 * half + 16] + found[32 + 16 * half : 48 + 16 * half]
+            pieces = []
             for k in range(4):
                 leaf = 64 * half + 8 * c + 2 * k
                 f0 = far[pl.ds(leaf, 8, stride=128), :]
@@ -532,28 +552,38 @@
                 gathered = jnp.concatenate(
                     [jnp.where(low8, f0, swap(f1)), jnp.where(low8, swap(f0), f1)], axis=0
                 )
-                to = pl.multiple_of(half * FLAT + c * 512 + k * 128, 128)
-                hats[:, pl.ds(to, 128)] = (block[:, 128 * k : 128 * k + 128] + gathered).astype(
-                    bf16
+                hat = (block[:, 128 * k : 128 * k + 128] + gathered).astype(bf16)
+                pieces.append(jnp.concatenate([hat * low16, hat * high16], axis=0))
+            for k in range(0, 4, 2):
+                leaf = 64 * half + 8 * c + 2 * k
+                stacked = jnp.concatenate(
+                    [
+                        jnp.concatenate([pieces[k], zero], axis=1),
+                        jnp.concatenate([zero, pieces[k + 1]], axis=1),
+                    ],
+                    axis=0,
                 )
-        return 0
-
-    lax.fori_loop(0, 8, hat_block, 0)
-    copies[2].wait()
-    copies[3].wait()
-
-    def leaf_block(i, _):
-        for k in range(8):
-            at = pl.multiple_of(i * 1024 + k * 128, 128)
-            hat = hats[:, pl.ds(at, 128)]
-            weight = basis[pl.ds(pl.multiple_of(i * 512 + k * 64, 64), 64), :]
-            found = mmt(jnp.concatenate([hat * low16, hat * high16], axis=0), weight)
-            out_ref[:, pl.ds(at, 128)] = (
-                jnp.concatenate([found[:NV], found[NV:]], axis=1) + near[:, pl.ds(at, 128)]
-            )
-        return 0
-
-    lax.fori_loop(0, 8, leaf_block, 0)
+                weight = jnp.concatenate(
+                    [
+                        basis[32 * leaf : 32 * leaf + 64, :],
+                        basis[32 * leaf + 64 : 32 * leaf + 128, :],
+                    ],
+                    axis=1,
+                )
+                part = mmt(stacked, weight)
+                for m in range(2):
+                    at = 64 * leaf + 128 * m
+                    out_ref[:, at : at + 128] = (
+                        jnp.concatenate(
+                            [part[32 * m : 32 * m + 16], part[32 * m + 16 : 32 * m + 32]], axis=1
+                        )
+                        + near[:, at : at + 128]
+                    )
+    edge = jnp.zeros((NV, HALF), f32)
+    out_ref[:, :128] += jnp.concatenate([mmt(before_ref[...], ends_ref[:, :HALF]), edge], axis=1)
+    out_ref[:, 8064:] += jnp.concatenate(
+        [edge, mmt(following_ref[...], ends_ref[:, HALF:])], axis=1
+    )
 
 
 def vmem():
@@ -614,9 +644,10 @@
             shape((LEAF_DEV * RANK // 2, 128), bf16),
             shape((LEAF_DEV * LEAF // 2, 128), bf16),
             shape((LEVELS, RANK, 128), bf16),
+            shape((LEAF, 128), bf16),
         ),
         in_specs=[vmem(), vmem(), vmem(), hbm(), hbm(), hbm(), vmem(), vmem()],
-        out_specs=(vmem(), vmem(), vmem(), vmem()),
+        out_specs=(vmem(), vmem(), vmem(), vmem(), vmem()),
         scratch_shapes=[
             pltpu.VMEM((LEAF_DEV, 3 * FLAT), bf16),
             pltpu.VMEM((LEAF_DEV, FLAT), bf16),
@@ -629,25 +660,19 @@
             pltpu.VMEM((128, 64, 128), bf16),
             pltpu.SemaphoreType.DMA((3,)),
         ],
-        compiler_params=params(60),
+        compiler_params=params(62),
         cost_estimate=pl.CostEstimate(
             flops=10**9, bytes_accessed=14 * 10**6, transcendentals=0
         ),
     )(after, xs, xe, near, basis, edges, top, couple)
 
 
-def run_down(got, near, down, basis, top):
+def run_down(got, near, down, basis, top, ends, before, following):
     return pl.pallas_call(
         down_kernel,
         name="down",
         out_shape=shape((NV, LEAF_DEV * LEAF), f32),
-        in_specs=[
-            pl.BlockSpec(memory_space=pl.ANY),
-            hbm(),
-            hbm(),
-            hbm(),
-            vmem(),
-        ],
+        in_specs=[hbm(), hbm(), hbm(), hbm(), vmem(), vmem(), vmem(), vmem()],
         out_specs=vmem(),
         scratch_shapes=[
             pltpu.VMEM((PEERS * TILES, 8, 128), bf16),
@@ -657,14 +682,13 @@
             pltpu.VMEM((PEERS * SLOTS * 8, 128), f32),
             pltpu.VMEM((PEERS * SLOTS, 128), f32),
             pltpu.VMEM((8 * LEAF_DEV, 128), f32),
-            pltpu.VMEM((NV, LEAF_DEV * LEAF), bf16),
-            pltpu.SemaphoreType.DMA((4,)),
+            pltpu.SemaphoreType.DMA((CHUNKS + 3,)),
         ],
         compiler_params=params(59),
         cost_estimate=pl.CostEstimate(
             flops=10**9, bytes_accessed=8 * 10**6, transcendentals=0
         ),
-    )(got, near, down, basis, top)
+    )(got, near, down, basis, top, ends, before, following)
 
 
 def shards(
@@ -679,27 +703,27 @@
     couple_owner,
     couple_dst,
 ):
-    ahead = [(i, (i + 1) % PEERS) for i in range(PEERS)]
-    back = [(target, source) for source, target in ahead]
-    before = lax.ppermute(x_vecs[:, -LEAF:], "leaf", ahead)
-    following = lax.ppermute(x_vecs[:, :LEAF], "leaf", back)
     top_flat = top_edges.reshape((LEVELS - 1) * 32, 128)
     outgoing, after = run_up(
         couple_src, couple_owner.reshape(PAIR_ROWS), couple_dst, x_vecs, leaf_basis,
         local_edges, top_flat, couple_blocks,
     )
-    outgoing, before, following = lax.optimization_barrier((outgoing, before, following))
+    first, last, after = lax.optimization_barrier((x_vecs[:, :LEAF], x_vecs[:, -LEAF:], after))
+    ahead = [(i, (i + 1) % PEERS) for i in range(PEERS)]
+    back = [(target, source) for source, target in ahead]
+    before = lax.ppermute(last, "leaf", ahead)
+    following = lax.ppermute(first, "leaf", back)
     got = lax.all_to_all(
         outgoing.reshape(PEERS, TILES * 8, 128), "leaf", split_axis=0, concat_axis=0, tiled=True
     ).reshape(PEERS * TILES, 8, 128)
     fill = jnp.zeros((NV, LEAF), bf16)
-    xs = jnp.concatenate([before, x_vecs, following], axis=1)
-    xe = jnp.concatenate([x_vecs, following, fill], axis=1)
-    near, down, basis, tops = run_mid(
+    xs = jnp.concatenate([fill, x_vecs, fill], axis=1)
+    xe = jnp.concatenate([x_vecs, fill, fill], axis=1)
+    near, down, basis, tops, ends = run_mid(
         after, xs, xe, near_blocks, leaf_basis, local_edges, top_flat,
         top_couple.reshape(LEVELS * 32, 128),
     )
-    return run_down(got, near, down, basis, tops)
+    return run_down(got, near, down, basis, tops, ends, before, following)
 
 
 def solution(mesh):

time: 80.3 us -> 70.2 us (0.87)
  waiting for transfers between devices: 16.3 us -> 8.66 us
  local copies, waits for them, and re-layouts: 4.06 us -> 1.75 us
  Pallas kernels: 42 us -> 40.4 us
  starting transfers between devices: 17.3 us -> 18.8 us
    all_to_all x1, waiting for transfers between devices: 16.3 us -> 1.04 us  [shards(): lax.all_to_all(outgoing.reshape(PEERS, TILES * 8, 128), 'leaf', split_axi...]
    ppermute x2, waiting for transfers between devices: 0.01 us -> 7.62 us  [the longest x1 7.62 us: shards(): before = lax.ppermute(last, 'leaf', ahead)]
    all_to_all x1, starting transfers between devices: 9.1 us -> 11.6 us  [shards(): lax.all_to_all(outgoing.reshape(PEERS, TILES * 8, 128), 'leaf', split_axi...]
    pallas_call x1, Pallas kernels: 8.44 us -> 6.7 us  [run_down(): pl.pallas_call(down_kernel, name='down', out_shape=shape((NV, LEAF_DEV *...]
    unnamed x4 -> x6, local copies, waits for them, and re-layouts: 1.52 us -> 0.01 us
    ppermute x2, starting transfers between devices: 8.21 us -> 7.18 us  [the longest x1 7.16 us: shards(): following = lax.ppermute(first, 'leaf', back)]
  transfers between devices with their start and end apart: 3 -> 3, of which waited for: 1 -> 2; matrix products, arithmetic and copies ran while one was open for 2% -> 2% of each run, Pallas kernels for 42% -> 26%
where the time goes in v3:
time: 70.2 us; the launch traced here: 69.6 us
  Pallas kernels  40.4 us (58%)
  starting transfers between devices  18.8 us (27%)
  waiting for transfers between devices  8.66 us (12%)
  local copies, waits for them, and re-layouts  1.75 us (2%)
    pallas_call x1, Pallas kernels, run_mid(): pl.pallas_call(mid_kernel, name='mid', out_shape=(shape((NV, LEAF_DEV * L...  18.3 us
    pallas_call x1, Pallas kernels, run_up(): pl.pallas_call(up_kernel, name='up', out_shape=(shape((PEERS * TILES, 8,...  15.4 us
    all_to_all x1, starting transfers between devices, shards(): lax.all_to_all(outgoing.reshape(PEERS, TILES * 8, 128), 'leaf', split_axi...  11.6 us
    ppermute x1, waiting for transfers between devices, shards(): before = lax.ppermute(last, 'leaf', ahead)  7.62 us
    ppermute x1, starting transfers between devices, shards(): following = lax.ppermute(first, 'leaf', back)  7.16 us
    pallas_call x1, Pallas kernels, run_down(): pl.pallas_call(down_kernel, name='down', out_shape=shape((NV, LEAF_DEV *...  6.7 us
  transfers between devices with their start and end apart: 3, of which 2 were waited for; matrix products, arithmetic and copies ran while one was open for 2% of the time, Pallas kernels for 26%

profile of v3, /device:TPU:0, one launch (start us, length us, event | category | flops | bytes accessed | tf_op | source)
XLA Modules:
  0.0 69.6 jit_solution(11892968117051246347)
XLA Ops:
  0.0 15.4 %up.1 = (bf16[1280,8,128]{2,1,0:T(8,128)(2,1)}, f32[8,128]{1,0:T(8,128)}) custom-call(bf16[16,8192]{1,0:T(8,128)(2,1)} %x_ref.1, f32[192,128]{1,0:T(8,128)} %bitcast.6, s32[512]{0:T(512)} %src_hbm.1, s32[512]{0:T(512)} %bitcast.9, s32[512]{0:T(512)} %dst_hbm.1, bf16[128,4096]{1,0:T(8,128)(2,1)} %basis_hbm.3, f32[254,4096]{1,0:T(8,128)} %edges_hbm.3, ...), custom_call_target="tpu_custom_call" | custom-call | flops 1000000000 | bytes 12000000 | tf_op jit(solution)/shard_map/up/pallas_call | solution.py:606
  15.4 0.0 copy-start
  15.4 11.6 %all-to-all-start = ((bf16[128,80,128]{2,1,0:T(8,128)(2,1)}), bf16[128,80,128]{2,1,0:T(8,128)(2,1)}, u32[]{:S(2)}, u32[]{:S(2)}) async-start(bf16[128,80,128]{2,1,0:T(8,128)(2,1)} %bitcast.5), calls=%async_computation | async-start | bytes 5242880 | tf_op jit(solution)/shard_map/all_to_all | solution.py:716
  27.0 0.0 copy-done
  27.1 0.1 fusion
  27.1 0.0 collective-permute-start
  27.2 7.2 %collective-permute-start.1 = (bf16[16,64]{1,0:T(8,128)(2,1)S(1)}, bf16[16,64]{1,0:T(8,128)(2,1)S(1)}, u32[]{:S(2)}, u32[]{:S(2)}) collective-permute-start(bf16[16,64]{1,0:T(8,128)(2,1)S(1)} %get-tuple-element.24), channel_id=1, source_target_pairs={{1,0},{2,1},{3,2},{4,3},{5,4},{6,5},{7,6},{8,7},{9,8},{10,9},{11,1... | collective-permute-start | bytes 6152 | tf_op jit(solution)/shard_map/ppermute | solution.py:715
  34.3 0.7 %concatenate.8.xe_ref = bf16[16,8320]{1,0:T(8,128)(2,1)} pad(bf16[16,8192]{1,0:T(8,128)(2,1)S(1)} %copy-done, bf16[]{:T(256)} %constant.1.clone.1), padding=0_0x0_128 | pad | bytes 528386 | tf_op jit(solution)/shard_map/concatenate | solution.py:721
  35.0 0.9 %concatenate.7.xs_ref = bf16[16,8320]{1,0:T(8,128)(2,1)} concatenate(bf16[16,64]{1,0:T(8,128)(2,1)S(1)} %broadcast_in_dim.3, bf16[16,8192]{1,0:T(8,128)(2,1)S(1)} %copy-done, bf16[16,64]{1,0:T(8,128)(2,1)S(1)} %broadcast_in_dim.3), dimensions={1} | concatenate | bytes 532480 | tf_op jit(solution)/shard_map/concatenate | solution.py:720
  36.0 18.3 %mid.1 = (f32[16,8192]{1,0:T(8,128)}, bf16[4096,128]{1,0:T(8,128)(2,1)}, bf16[4096,128]{1,0:T(8,128)(2,1)}, bf16[7,64,128]{2,1,0:T(8,128)(2,1)}, bf16[64,128]{1,0:T(8,128)(2,1)}) custom-call(f32[8,128]{1,0:T(8,128)} %get-tuple-element.17.after_ref, bf16[16,8320]{1,0:T(8,128)(2,1)} %concatenate.7.xs_ref, bf16[16,8320]{1,0:T(8,128)(2,1)} %concatenate.8.xe_ref, ...), custom_call_target="tpu_custom_call" | custom-call | flops 1000000000 | bytes 14000000 | tf_op jit(solution)/shard_map/mid/pallas_call | solution.py:639
  54.2 7.6 %collective-permute-done.before_ref = bf16[16,64]{1,0:T(8,128)(2,1)S(1)} collective-permute-done((bf16[16,64]{1,0:T(8,128)(2,1)S(1)}, bf16[16,64]{1,0:T(8,128)(2,1)S(1)}, u32[]{:S(2)}, u32[]{:S(2)}) %collective-permute-start) | collective-permute-done | bytes 2080 | tf_op jit(solution)/shard_map/ppermute | solution.py:714
  61.9 0.0 copy-start.1
  61.9 0.0 collective-permute-done.1.following_ref
  61.9 0.0 copy-start.2
  61.9 1.0 %all-to-all-done = bf16[128,80,128]{2,1,0:T(8,128)(2,1)} async-done(((bf16[128,80,128]{2,1,0:T(8,128)(2,1)}), bf16[128,80,128]{2,1,0:T(8,128)(2,1)}, u32[]{:S(2)}, u32[]{:S(2)}) %all-to-all-start) | async-done | bytes 2621472 | tf_op jit(solution)/shard_map/all_to_all | solution.py:716
  62.9 0.0 copy-done.1
  62.9 0.0 copy-done.2
  62.9 6.7 %down.1 = f32[16,8192]{1,0:T(8,128)} custom-call(bf16[1280,8,128]{2,1,0:T(8,128)(2,1)} %bitcast.3.got_hbm, f32[16,8192]{1,0:T(8,128)} %get-tuple-element.18.near_hbm, bf16[4096,128]{1,0:T(8,128)(2,1)} %get-tuple-element.19.down_hbm, bf16[4096,128]{1,0:T(8,128)(2,1)} %get-tuple-element.20.basis_hbm, bf16[7,64,128]{2,1,0:T(8,128)(2,1)} %get-tuple-element.21.top_ref, ...), custom_call_target="tpu_custom_call" | custom-call | flops 1000000000 | bytes 8000000 | tf_op jit(solution)/shard_map/down/pallas_call | solution.py:671
  (1 shorter events, 0.0 us)
Async XLA Ops:
  15.4 11.6 %copy-start = (bf16[16,8192]{1,0:T(8,128)(2,1)S(1)}, bf16[16,8192]{1,0:T(8,128)(2,1)}, u32[]{:S(2)}) copy-start(bf16[16,8192]{1,0:T(8,128)(2,1)} %x_ref.1) | copy-start | bytes 786436
  15.4 47.5 %all-to-all-start = ((bf16[128,80,128]{2,1,0:T(8,128)(2,1)}), bf16[128,80,128]{2,1,0:T(8,128)(2,1)}, u32[]{:S(2)}, u32[]{:S(2)}) async-start(bf16[128,80,128]{2,1,0:T(8,128)(2,1)} %bitcast.5), calls=%async_computation | async-start | bytes 5242880 | tf_op jit(solution)/shard_map/all_to_all | solution.py:716
  27.1 34.7 %collective-permute-start = (bf16[16,64]{1,0:T(8,128)(2,1)S(1)}, bf16[16,64]{1,0:T(8,128)(2,1)S(1)}, u32[]{:S(2)}, u32[]{:S(2)}) collective-permute-start(bf16[16,64]{1,0:T(8,128)(2,1)S(1)} %get-tuple-element.23), channel_id=1, source_target_pairs={{0,1},{1,2},{2,3},{3,4},{4,5},{5,6},{6,7},{7,8},{8,9},{9,10},{10,1... | collective-permute-start | bytes 6152 | tf_op jit(solution)/shard_map/ppermute | solution.py:714
  27.2 34.7 %collective-permute-start.1 = (bf16[16,64]{1,0:T(8,128)(2,1)S(1)}, bf16[16,64]{1,0:T(8,128)(2,1)S(1)}, u32[]{:S(2)}, u32[]{:S(2)}) collective-permute-start(bf16[16,64]{1,0:T(8,128)(2,1)S(1)} %get-tuple-element.24), channel_id=1, source_target_pairs={{1,0},{2,1},{3,2},{4,3},{5,4},{6,5},{7,6},{8,7},{9,8},{10,9},{11,1... | collective-permute-start | bytes 6152 | tf_op jit(solution)/shard_map/ppermute | solution.py:715
  61.9 1.1 %copy-start.1 = (bf16[16,64]{1,0:T(8,128)(2,1)}, bf16[16,64]{1,0:T(8,128)(2,1)S(1)}, u32[]{:S(2)}) copy-start(bf16[16,64]{1,0:T(8,128)(2,1)S(1)} %collective-permute-done.before_ref) | copy-start | bytes 6148
  61.9 1.0 %copy-start.2 = (bf16[16,64]{1,0:T(8,128)(2,1)}, bf16[16,64]{1,0:T(8,128)(2,1)S(1)}, u32[]{:S(2)}) copy-start(bf16[16,64]{1,0:T(8,128)(2,1)S(1)} %collective-permute-done.1.following_ref) | copy-start | bytes 6148

commit v4 on v3

--- a/solution.py
+++ b/solution.py
@@ -65,6 +65,18 @@
         stage[pl.ds((2 * j + 1) * group, group), :] = jnp.where(low, swap(first), second)
 
 
+def paired_half(stage, load_first, load_second):
+    for j in range(32):
+        first = load_first(j)
+        second = load_second(j)
+        stage[pl.ds(32 * j, 16), :] = jnp.concatenate(
+            [first[:, :HALF], second[:, :HALF]], axis=1
+        ).astype(f32)
+        stage[pl.ds(32 * j + 16, 16), :] = jnp.concatenate(
+            [first[:, HALF:], second[:, HALF:]], axis=1
+        ).astype(f32)
+
+
 def matrix(stage, group, index):
     return stage[pl.ds(index, 64, stride=group), :]
 
@@ -73,19 +85,25 @@
     return pl.ds(start + j * 128, 128)
 
 
-def relayout_edges(edges, stage, stage_two, highs, lows):
+def edge_steps(edges, stage, stage_two, highs, lows):
     def keep(at, index, place):
         high, low = split(matrix(at, 8, index))
         highs[place] = high
         lows[place] = low
 
     def layout(g, to):
-        first = jnp.where(
-            g < 8, 8 * g, jnp.where(g < 12, 64 + 8 * g, jnp.where(g < 14, 96 + 8 * g, 224))
-        )
-        gap = jnp.where(g < 8, 64, jnp.where(g < 12, 32, jnp.where(g < 14, 16, 8)))
-        first = pl.multiple_of(first, 8)
-        second = pl.multiple_of(first + gap, 8)
+        if isinstance(g, int):
+            first, gap = 8 * g, 64
+            if g >= 8:
+                first, gap = (64 + 8 * g, 32) if g < 12 else (96 + 8 * g, 16) if g < 14 else (224, 8)
+            second = first + gap
+        else:
+            first = jnp.where(
+                g < 8, 8 * g, jnp.where(g < 12, 64 + 8 * g, jnp.where(g < 14, 96 + 8 * g, 224))
+            )
+            gap = jnp.where(g < 8, 64, jnp.where(g < 12, 32, jnp.where(g < 14, 16, 8)))
+            first = pl.multiple_of(first, 8)
+            second = pl.multiple_of(first + gap, 8)
         paired(
             to,
             8,
@@ -93,17 +111,24 @@
             lambda j: edges[pl.ds(second, 8), lanes(j)],
         )
 
-    def step(h, _):
-        odd = jnp.minimum(2 * h + 1, 14)
+    def step(h):
+        odd = min(2 * h + 1, 14) if isinstance(h, int) else jnp.minimum(2 * h + 1, 14)
         layout(2 * h, stage)
-        layout(odd, stage_two)
+        if not (isinstance(h, int) and h == 7):
+            layout(odd, stage_two)
         for i in range(8):
             keep(stage, i, 16 * h + i)
-        for i in range(8):
-            keep(stage_two, i, 8 * odd + i)
-        return 0
-
-    lax.fori_loop(0, 8, step, 0)
+        if not (isinstance(h, int) and h == 7):
+            for i in range(8):
+                keep(stage_two, i, 8 * odd + i)
+
+    def last():
+        last_levels(edges, stage, stage_two, keep)
+
+    return step, last
+
+
+def last_levels(edges, stage, stage_two, keep):
     paired(
         stage,
         8,
@@ -124,23 +149,48 @@
     keep(stage_two, 6, 126)
 
 
+def relayout_edges(edges, stage, stage_two, highs, lows):
+    step, last = edge_steps(edges, stage, stage_two, highs, lows)
+
+    def body(h, _):
+        step(h)
+        return 0
+
+    lax.fori_loop(0, 8, body, 0)
+    last()
+
+
 def up_kernel(
-    x_ref, top_ref, src_hbm, own_hbm, dst_hbm, basis_hbm, edges_hbm, pairs_hbm,
+    x_ref, top_ref, own_ref, dst_ref, src_hbm, basis_hbm, edges_hbm, pairs_hbm,
     out_ref, done_ref,
-    src_ref, own_ref, dst_ref, basis, edges, pairs, stage, stage_two, tops, vec_a, vec_b,
-    highs, lows, table, rows_at, count, sems,
+    src_ref, tile_ref, basis, edges, pairs, stage, stage_two, stage_three, stage_four, tops, vec_a, vec_b,
+    highs, lows, table, tile_at, sems,
 ):
     basis_copy = pltpu.make_async_copy(basis_hbm, basis, sems.at[0])
-    edges_copy = pltpu.make_async_copy(edges_hbm, edges, sems.at[1])
-    pairs_copy = pltpu.make_async_copy(pairs_hbm, pairs, sems.at[2])
-    lists = [
-        pltpu.make_async_copy(src_hbm, src_ref, sems.at[3]),
-        pltpu.make_async_copy(own_hbm, own_ref, sems.at[4]),
-        pltpu.make_async_copy(dst_hbm, dst_ref, sems.at[5]),
+    pair_copies = [
+        pltpu.make_async_copy(
+            pairs_hbm.at[pl.ds(128 * c, 128)], pairs.at[pl.ds(128 * c, 128)], sems.at[5 + c]
+        )
+        for c in range(4)
     ]
+    edge_copies = [
+        pltpu.make_async_copy(
+            edges_hbm.at[pl.ds(0, 128)], edges.at[pl.ds(0, 128)], sems.at[1]
+        ),
+        pltpu.make_async_copy(
+            edges_hbm.at[pl.ds(128, EDGE_ROWS - 128)],
+            edges.at[pl.ds(128, EDGE_ROWS - 128)],
+            sems.at[2],
+        ),
+    ]
+    source_copy = pltpu.make_async_copy(src_hbm, src_ref, sems.at[3])
+    tile_copy = pltpu.make_async_copy(tile_at, tile_ref, sems.at[4])
     basis_copy.start()
-    edges_copy.start()
-    for copy in lists:
+    source_copy.start()
+    for copy in (
+        pair_copies[0], edge_copies[0], pair_copies[1], edge_copies[1], pair_copies[2],
+        pair_copies[3],
+    ):
         copy.start()
     low16, high16 = half_masks(16)
     low = low_lanes(16)
@@ -150,30 +200,58 @@
         return 0
 
     lax.fori_loop(0, PEERS * TILES // 32, clear, 0)
-    rows_at[...] = jnp.zeros_like(rows_at)
-
-    def clear_count(i, _):
+
+    blocks = PAIR_ROWS // 128
+    sub = lax.broadcasted_iota(jnp.int32, (128, 128), 0)
+    lane = lax.broadcasted_iota(jnp.int32, (128, 128), 1)
+    across = [
+        jnp.broadcast_to(own_ref[b : b + 1, :].astype(f32), (128, 128)) for b in range(blocks)
+    ]
+    along = [value.T for value in across]
+    wanted = jnp.concatenate(
+        [
+            jnp.where(
+                jnp.broadcast_to(dst_ref[b : b + 1, :].astype(f32), (128, 128)).T
+                == lane.astype(f32),
+                1.0,
+                0.0,
+            )
+            for b in range(blocks)
+        ],
+        axis=0,
+    ).astype(bf16)
+    slots = []
+    for c in range(blocks):
+        same = jnp.where((along[c] == across[c]) & (sub < lane), 1.0, 0.0)
+        for b in range(c):
+            same = same + jnp.where(along[b] == across[c], 1.0, 0.0)
+        rank = jnp.sum(same, axis=0, keepdims=True)
+        tile_at[c : c + 1, :] = (across[c][0:1] * TILES + rank).astype(jnp.int32)
+        slots.append(jnp.broadcast_to(across[c][0:1] * SLOTS + rank, (128, 128)))
+    tile_copy.start()
+    for m in range(SLOTS):
+        here = (sub + 128 * m).astype(f32)
+        placing = jnp.concatenate(
+            [jnp.where(slot == here, 1.0, 0.0) for slot in slots], axis=1
+        ).astype(bf16)
+        rows = mm(placing, wanted)
         for k in range(16):
-            count[16 * i + k] = 0
-        return 0
-
-    lax.fori_loop(0, PEERS // 16, clear_count, 0)
+            out_ref[(16 * m + k) * TILES + SLOTS + 1] = rows[8 * k : 8 * k + 8].astype(bf16)
+
     for level in range(LEVELS - 1):
         tile = top_ref[32 * level : 32 * level + 32, :]
         tops[pl.ds(64 * level, 32, stride=2), :] = tile
         tops[pl.ds(64 * level + 1, 32, stride=2), :] = swap(tile)
 
     basis_copy.wait()
-    pairs_copy.start()
 
     def leaf_layout(g, to):
         first = pl.multiple_of(16 * g, 16)
         second = pl.multiple_of(64 + 16 * g, 16)
-        paired(
+        paired_half(
             to,
-            16,
-            lambda j: basis[pl.ds(first, 16), lanes(j)].astype(f32),
-            lambda j: basis[pl.ds(second, 16), lanes(j)].astype(f32),
+            lambda j: basis[pl.ds(first, 16), lanes(j)],
+            lambda j: basis[pl.ds(second, 16), lanes(j)],
         )
 
     def leaf_products(g, at_stage):
@@ -203,8 +281,7 @@
 
     lax.fori_loop(0, 2, leaf_step, 0)
 
-    edges_copy.wait()
-    relayout_edges(edges, stage, stage_two, highs, lows)
+    edge_step, edge_last = edge_steps(edges, stage_three, stage_four, highs, lows)
 
     def parents(nodes, first, amount):
         up = nodes in (128, 32, 8)
@@ -245,23 +322,23 @@
         for x in range(2**level, 2 ** (level + 1)):
             out_ref[lax.bitwise_xor(me, x) * TILES + SLOTS] = tile
 
-    for copy in lists:
-        copy.wait()
-    pairs_copy.wait()
-    lane_ids = lax.broadcasted_iota(jnp.int32, (1, 128), 1)
+    source_copy.wait()
+    tile_copy.wait()
+    pair_copies[0].wait()
 
     def pair_layout(g, to):
         first = pl.multiple_of(32 * g, 16)
         second = pl.multiple_of(32 * g + 16, 16)
-        paired(
+        paired_half(
             to,
-            16,
-            lambda j: pairs[pl.ds(first, 16), lanes(j)].astype(f32),
-            lambda j: pairs[pl.ds(second, 16), lanes(j)].astype(f32),
+            lambda j: pairs[pl.ds(first, 16), lanes(j)],
+            lambda j: pairs[pl.ds(second, 16), lanes(j)],
         )
 
     def pair_products(g, at):
         zero = jnp.zeros((32, 128), bf16)
+        row = g // 4
+        column = 32 * (g % 4)
         for i in range(0, 16, 2):
             weight = jnp.concatenate(
                 [matrix(at, 16, i), matrix(at, 16, i + 1)], axis=1
@@ -279,16 +356,10 @@
             )
             found = mmt(stacked, weight)
             for k in range(4):
-                owner = own_ref[listed[k]]
-                rank = count[owner]
-                count[owner] = rank + 1
                 tile = jnp.concatenate(
                     [found[16 * k : 16 * k + 8], found[16 * k + 8 : 16 * k + 16]], axis=1
                 )
-                out_ref[owner * TILES + rank] = tile.astype(bf16)
-                rows_at[pl.ds(owner * SLOTS + rank, 1), :] = jnp.where(
-                    lane_ids == dst_ref[listed[k]], 1.0, 0.0
-                )
+                out_ref[tile_ref[row, column + listed[k] - 32 * g]] = tile.astype(bf16)
 
     groups = PAIR_ROWS // 32
     pair_layout(0, stage)
@@ -296,39 +367,49 @@
     def pair_step(h):
         pair_layout(2 * h + 1, stage_two)
         pair_products(2 * h, stage)
-        pair_layout(jnp.minimum(2 * h + 2, groups - 1), stage)
+        if 2 * h + 2 < groups:
+            pair_layout(2 * h + 2, stage)
         pair_products(2 * h + 1, stage_two)
 
-    def first_steps(h, _):
-        parents(128, 8 * h, 8)
-        pair_step(h)
-        return 0
-
-    lax.fori_loop(0, 4, first_steps, 0)
+    edge_copies[0].wait()
+    edge_step(0)
+    edge_step(1)
+    pair_step(0)
+    pair_copies[1].wait()
+    edge_step(2)
+    edge_step(3)
+    parents(128, 0, 16)
+    pair_step(1)
+    edge_copies[1].wait()
+    edge_step(4)
+    edge_step(5)
+    parents(128, 16, 16)
+    pair_step(2)
+    pair_copies[2].wait()
+    edge_step(6)
+    edge_step(7)
+    edge_last()
     parents(64, 0, 16)
-    pair_step(4)
+    pair_step(3)
     parents(32, 0, 8)
     parents(16, 0, 4)
-    pair_step(5)
+    pair_step(4)
+    pair_copies[3].wait()
     parents(8, 0, 2)
     parents(4, 0, 1)
     current = root()
     send(current, 0)
     current = carried(current, 0)
+    pair_step(5)
+    for level in range(1, 3):
+        send(current, level)
+        current = carried(current, level)
     pair_step(6)
-    for level in range(1, LEVELS):
+    for level in range(3, LEVELS):
         send(current, level)
         if level < LEVELS - 1:
             current = carried(current, level)
     pair_step(7)
-
-    def place_rows(o, _):
-        out_ref[o * TILES + SLOTS + 1] = rows_at[
-            pl.ds(pl.multiple_of(o * SLOTS, 8), 8), :
-        ].astype(bf16)
-        return 0
-
-    lax.fori_loop(0, PEERS, place_rows, 0, unroll=16)
     done_ref[...] = current[0:8]
 
 
@@ -497,10 +578,10 @@
 
     for c in range(CHUNKS):
         arriving[c].wait()
-        if c == CHUNKS - 2:
+        if c == 0:
             for copy in copies:
                 copy.start()
-        lax.fori_loop(c * span, (c + 1) * span, unpack, 0, unroll=4)
+        lax.fori_loop(c * span, (c + 1) * span, unpack, 0, unroll=8)
     landing = jnp.concatenate(
         [target[128 * i : 128 * i + 128, :].T for i in range(SLOTS)], axis=1
     ).astype(bf16)
@@ -607,32 +688,32 @@
         up_kernel,
         name="up",
         out_shape=(shape((PEERS * TILES, 8, 128), bf16), shape((8, 128), f32)),
-        in_specs=[vmem(), vmem(), hbm(), hbm(), hbm(), hbm(), hbm(), hbm()],
+        in_specs=[vmem(), vmem(), vmem(), vmem(), hbm(), hbm(), hbm(), hbm()],
         out_specs=(vmem(), vmem()),
         scratch_shapes=[
             pltpu.SMEM((PAIR_ROWS,), jnp.int32),
-            pltpu.SMEM((PAIR_ROWS,), jnp.int32),
-            pltpu.SMEM((PAIR_ROWS,), jnp.int32),
+            pltpu.SMEM((PAIR_ROWS // 128, 128), jnp.int32),
             pltpu.VMEM((LEAF_DEV, FLAT), bf16),
             pltpu.VMEM((EDGE_ROWS, FLAT), f32),
             pltpu.VMEM((PAIR_ROWS, FLAT), bf16),
             pltpu.VMEM((1024, 128), f32),
             pltpu.VMEM((1024, 128), f32),
+            pltpu.VMEM((512, 128), f32),
+            pltpu.VMEM((512, 128), f32),
             pltpu.VMEM((64 * (LEVELS - 1), 128), f32),
             pltpu.VMEM((64, NV, 128), f32),
             pltpu.VMEM((64, NV, 128), f32),
             pltpu.VMEM((128, 64, 128), bf16),
             pltpu.VMEM((128, 64, 128), bf16),
             pltpu.VMEM((LEAF_DEV, NV, 128), bf16),
-            pltpu.VMEM((PEERS * SLOTS, 128), f32),
-            pltpu.SMEM((PEERS,), jnp.int32),
-            pltpu.SemaphoreType.DMA((6,)),
+            pltpu.VMEM((PAIR_ROWS // 128, 128), jnp.int32),
+            pltpu.SemaphoreType.DMA((9,)),
         ],
         compiler_params=params(60),
         cost_estimate=pl.CostEstimate(
             flops=10**9, bytes_accessed=12 * 10**6, transcendentals=0
         ),
-    )(x_vecs, top_edges, src, own, dst, basis, edges, pairs)
+    )(x_vecs, top_edges, own, dst, src, basis, edges, pairs)
 
 
 def run_mid(after, xs, xe, near, basis, edges, top, couple):
@@ -705,8 +786,9 @@
 ):
     top_flat = top_edges.reshape((LEVELS - 1) * 32, 128)
     outgoing, after = run_up(
-        couple_src, couple_owner.reshape(PAIR_ROWS), couple_dst, x_vecs, leaf_basis,
-        local_edges, top_flat, couple_blocks,
+        couple_src, couple_owner.reshape(PAIR_ROWS // 128, 128),
+        couple_dst.reshape(PAIR_ROWS // 128, 128), x_vecs, leaf_basis, local_edges, top_flat,
+        couple_blocks,
     )
     first, last, after = lax.optimization_barrier((x_vecs[:, :LEAF], x_vecs[:, -LEAF:], after))
     ahead = [(i, (i + 1) % PEERS) for i in range(PEERS)]

time: 70.2 us -> 67.4 us (0.960)
  Pallas kernels: 40.4 us -> 37.4 us
    pallas_call x1, Pallas kernels: 15.4 us -> 12.7 us  [run_up(): pl.pallas_call(up_kernel, name='up', out_shape=(shape((PEERS * TILES, 8,...]
  transfers between devices with their start and end apart: 3 -> 3, of which waited for: 2 -> 2; matrix products, arithmetic and copies ran while one was open for 2% -> 3% of each run, Pallas kernels for 26% -> 27%
where the time goes in v4:
time: 67.4 us; the launch traced here: 66.8 us
  Pallas kernels  37.4 us (55%)
  starting transfers between devices  18.9 us (28%)
  waiting for transfers between devices  8.58 us (13%)
  local copies, waits for them, and re-layouts  1.75 us (3%)
    pallas_call x1, Pallas kernels, run_mid(): pl.pallas_call(mid_kernel, name='mid', out_shape=(shape((NV, LEAF_DEV * L...  18.3 us
    pallas_call x1, Pallas kernels, run_up(): pl.pallas_call(up_kernel, name='up', out_shape=(shape((PEERS * TILES, 8,...  12.7 us
    all_to_all x1, starting transfers between devices, shards(): lax.all_to_all(outgoing.reshape(PEERS, TILES * 8, 128), 'leaf', split_axi...  11.6 us
    ppermute x1, waiting for transfers between devices, shards(): before = lax.ppermute(last, 'leaf', ahead)  7.54 us
    ppermute x1, starting transfers between devices, shards(): following = lax.ppermute(first, 'leaf', back)  7.24 us
    pallas_call x1, Pallas kernels, run_down(): pl.pallas_call(down_kernel, name='down', out_shape=shape((NV, LEAF_DEV *...  6.41 us
  transfers between devices with their start and end apart: 3, of which 2 were waited for; matrix products, arithmetic and copies ran while one was open for 3% of the time, Pallas kernels for 27%

profile of v4, /device:TPU:0, one launch (start us, length us, event | category | flops | bytes accessed | tf_op | source)
XLA Modules:
  0.0 66.8 jit_solution(10296175754762509227)
XLA Ops:
  0.0 12.7 %up.1 = (bf16[1280,8,128]{2,1,0:T(8,128)(2,1)}, f32[8,128]{1,0:T(8,128)}) custom-call(bf16[16,8192]{1,0:T(8,128)(2,1)} %x_ref.1, f32[192,128]{1,0:T(8,128)} %bitcast.7, s32[4,128]{1,0:T(4,128)} %bitcast.10, s32[4,128]{1,0:T(4,128)} %bitcast.11, s32[512]{0:T(512)} %src_hbm.1, bf16[128,4096]{1,0:T(8,128)(2,1)} %basis_hbm.3, f32[254,4096]{1,0:T(8,128)} %edges_hbm.3, ...), custom_call_target="tpu_custom_call" | custom-call | flops 1000000000 | bytes 12000000 | tf_op jit(solution)/shard_map/up/pallas_call | solution.py:687
  12.8 0.0 copy-start
  12.8 11.6 %all-to-all-start = ((bf16[128,80,128]{2,1,0:T(8,128)(2,1)}), bf16[128,80,128]{2,1,0:T(8,128)(2,1)}, u32[]{:S(2)}, u32[]{:S(2)}) async-start(bf16[128,80,128]{2,1,0:T(8,128)(2,1)} %bitcast.6), calls=%async_computation | async-start | bytes 5242880 | tf_op jit(solution)/shard_map/all_to_all | solution.py:798
  24.4 0.0 copy-done
  24.4 0.1 fusion
  24.5 0.0 collective-permute-start
  24.5 7.2 %collective-permute-start.1 = (bf16[16,64]{1,0:T(8,128)(2,1)S(1)}, bf16[16,64]{1,0:T(8,128)(2,1)S(1)}, u32[]{:S(2)}, u32[]{:S(2)}) collective-permute-start(bf16[16,64]{1,0:T(8,128)(2,1)S(1)} %get-tuple-element.24), channel_id=1, source_target_pairs={{1,0},{2,1},{3,2},{4,3},{5,4},{6,5},{7,6},{8,7},{9,8},{10,9},{11,1... | collective-permute-start | bytes 6152 | tf_op jit(solution)/shard_map/ppermute | solution.py:797
  31.7 0.7 %concatenate.8.xe_ref = bf16[16,8320]{1,0:T(8,128)(2,1)} pad(bf16[16,8192]{1,0:T(8,128)(2,1)S(1)} %copy-done, bf16[]{:T(256)} %constant.1.clone.1), padding=0_0x0_128 | pad | bytes 528386 | tf_op jit(solution)/shard_map/concatenate | solution.py:803
  32.5 0.9 %concatenate.7.xs_ref = bf16[16,8320]{1,0:T(8,128)(2,1)} concatenate(bf16[16,64]{1,0:T(8,128)(2,1)S(1)} %broadcast_in_dim.3, bf16[16,8192]{1,0:T(8,128)(2,1)S(1)} %copy-done, bf16[16,64]{1,0:T(8,128)(2,1)S(1)} %broadcast_in_dim.3), dimensions={1} | concatenate | bytes 532480 | tf_op jit(solution)/shard_map/concatenate | solution.py:802
  33.4 18.3 %mid.1 = (f32[16,8192]{1,0:T(8,128)}, bf16[4096,128]{1,0:T(8,128)(2,1)}, bf16[4096,128]{1,0:T(8,128)(2,1)}, bf16[7,64,128]{2,1,0:T(8,128)(2,1)}, bf16[64,128]{1,0:T(8,128)(2,1)}) custom-call(f32[8,128]{1,0:T(8,128)} %get-tuple-element.17.after_ref, bf16[16,8320]{1,0:T(8,128)(2,1)} %concatenate.7.xs_ref, bf16[16,8320]{1,0:T(8,128)(2,1)} %concatenate.8.xe_ref, ...), custom_call_target="tpu_custom_call" | custom-call | flops 1000000000 | bytes 14000000 | tf_op jit(solution)/shard_map/mid/pallas_call | solution.py:720
  51.7 7.5 %collective-permute-done.before_ref = bf16[16,64]{1,0:T(8,128)(2,1)S(1)} collective-permute-done((bf16[16,64]{1,0:T(8,128)(2,1)S(1)}, bf16[16,64]{1,0:T(8,128)(2,1)S(1)}, u32[]{:S(2)}, u32[]{:S(2)}) %collective-permute-start) | collective-permute-done | bytes 2080 | tf_op jit(solution)/shard_map/ppermute | solution.py:796
  59.2 0.0 copy-start.1
  59.2 0.0 collective-permute-done.1.following_ref
  59.2 0.0 copy-start.2
  59.2 1.0 %all-to-all-done = bf16[128,80,128]{2,1,0:T(8,128)(2,1)} async-done(((bf16[128,80,128]{2,1,0:T(8,128)(2,1)}), bf16[128,80,128]{2,1,0:T(8,128)(2,1)}, u32[]{:S(2)}, u32[]{:S(2)}) %all-to-all-start) | async-done | bytes 2621472 | tf_op jit(solution)/shard_map/all_to_all | solution.py:798
  60.3 0.0 copy-done.1
  60.3 0.0 copy-done.2
  60.3 6.4 %down.1 = f32[16,8192]{1,0:T(8,128)} custom-call(bf16[1280,8,128]{2,1,0:T(8,128)(2,1)} %bitcast.4.got_hbm, f32[16,8192]{1,0:T(8,128)} %get-tuple-element.18.near_hbm, bf16[4096,128]{1,0:T(8,128)(2,1)} %get-tuple-element.19.down_hbm, bf16[4096,128]{1,0:T(8,128)(2,1)} %get-tuple-element.20.basis_hbm, bf16[7,64,128]{2,1,0:T(8,128)(2,1)} %get-tuple-element.21.top_ref, ...), custom_call_target="tpu_custom_call" | custom-call | flops 1000000000 | bytes 8000000 | tf_op jit(solution)/shard_map/down/pallas_call | solution.py:752
  (1 shorter events, 0.0 us)
Async XLA Ops:
  12.8 11.6 %copy-start = (bf16[16,8192]{1,0:T(8,128)(2,1)S(1)}, bf16[16,8192]{1,0:T(8,128)(2,1)}, u32[]{:S(2)}) copy-start(bf16[16,8192]{1,0:T(8,128)(2,1)} %x_ref.1) | copy-start | bytes 786436
  12.8 47.5 %all-to-all-start = ((bf16[128,80,128]{2,1,0:T(8,128)(2,1)}), bf16[128,80,128]{2,1,0:T(8,128)(2,1)}, u32[]{:S(2)}, u32[]{:S(2)}) async-start(bf16[128,80,128]{2,1,0:T(8,128)(2,1)} %bitcast.6), calls=%async_computation | async-start | bytes 5242880 | tf_op jit(solution)/shard_map/all_to_all | solution.py:798
  24.5 34.7 %collective-permute-start = (bf16[16,64]{1,0:T(8,128)(2,1)S(1)}, bf16[16,64]{1,0:T(8,128)(2,1)S(1)}, u32[]{:S(2)}, u32[]{:S(2)}) collective-permute-start(bf16[16,64]{1,0:T(8,128)(2,1)S(1)} %get-tuple-element.23), channel_id=1, source_target_pairs={{0,1},{1,2},{2,3},{3,4},{4,5},{5,6},{6,7},{7,8},{8,9},{9,10},{10,1... | collective-permute-start | bytes 6152 | tf_op jit(solution)/shard_map/ppermute | solution.py:796
  24.5 34.7 %collective-permute-start.1 = (bf16[16,64]{1,0:T(8,128)(2,1)S(1)}, bf16[16,64]{1,0:T(8,128)(2,1)S(1)}, u32[]{:S(2)}, u32[]{:S(2)}) collective-permute-start(bf16[16,64]{1,0:T(8,128)(2,1)S(1)} %get-tuple-element.24), channel_id=1, source_target_pairs={{1,0},{2,1},{3,2},{4,3},{5,4},{6,5},{7,6},{8,7},{9,8},{10,9},{11,1... | collective-permute-start | bytes 6152 | tf_op jit(solution)/shard_map/ppermute | solution.py:797
  59.2 1.1 %copy-start.1 = (bf16[16,64]{1,0:T(8,128)(2,1)}, bf16[16,64]{1,0:T(8,128)(2,1)S(1)}, u32[]{:S(2)}) copy-start(bf16[16,64]{1,0:T(8,128)(2,1)S(1)} %collective-permute-done.before_ref) | copy-start | bytes 6148
  59.2 1.0 %copy-start.2 = (bf16[16,64]{1,0:T(8,128)(2,1)}, bf16[16,64]{1,0:T(8,128)(2,1)S(1)}, u32[]{:S(2)}) copy-start(bf16[16,64]{1,0:T(8,128)(2,1)S(1)} %collective-permute-done.1.following_ref) | copy-start | bytes 6148

commit v5 on v4

--- a/solution.py
+++ b/solution.py
@@ -272,14 +272,14 @@
                 table[t] = jnp.where(low, pair, turned).astype(bf16)
                 table[t + 64] = jnp.where(low, turned, pair).astype(bf16)
 
-    def leaf_step(h, _):
+    def leaf_step(h):
         leaf_layout(2 * h, stage)
         leaf_layout(2 * h + 1, stage_two)
         leaf_products(2 * h, stage)
         leaf_products(2 * h + 1, stage_two)
-        return 0
-
-    lax.fori_loop(0, 2, leaf_step, 0)
+
+    leaf_step(0)
+    leaf_step(1)
 
     edge_step, edge_last = edge_steps(edges, stage_three, stage_four, highs, lows)
 

time: 67.4 us -> 67.2 us (level)
  no operation moved by 1% of the time
where the time goes in v5:
time: 67.2 us; the launch traced here: 66.7 us
  Pallas kernels  37.2 us (55%)
  starting transfers between devices  18.9 us (28%)
  waiting for transfers between devices  8.58 us (13%)
  local copies, waits for them, and re-layouts  1.75 us (3%)
    pallas_call x1, Pallas kernels, run_mid(): pl.pallas_call(mid_kernel, name='mid', out_shape=(shape((NV, LEAF_DEV * L...  18.3 us
    pallas_call x1, Pallas kernels, run_up(): pl.pallas_call(up_kernel, name='up', out_shape=(shape((PEERS * TILES, 8,...  12.6 us
    all_to_all x1, starting transfers between devices, shards(): lax.all_to_all(outgoing.reshape(PEERS, TILES * 8, 128), 'leaf', split_axi...  11.6 us
    ppermute x1, waiting for transfers between devices, shards(): before = lax.ppermute(last, 'leaf', ahead)  7.54 us
    ppermute x1, starting transfers between devices, shards(): following = lax.ppermute(first, 'leaf', back)  7.24 us
    pallas_call x1, Pallas kernels, run_down(): pl.pallas_call(down_kernel, name='down', out_shape=shape((NV, LEAF_DEV *...  6.41 us
  transfers between devices with their start and end apart: 3, of which 2 were waited for; matrix products, arithmetic and copies ran while one was open for 3% of the time, Pallas kernels for 27%

profile of v5, /device:TPU:0, one launch (start us, length us, event | category | flops | bytes accessed | tf_op | source)
XLA Modules:
  0.0 66.7 jit_solution(7404210679881242269)
XLA Ops:
  0.0 12.6 %up.1 = (bf16[1280,8,128]{2,1,0:T(8,128)(2,1)}, f32[8,128]{1,0:T(8,128)}) custom-call(bf16[16,8192]{1,0:T(8,128)(2,1)} %x_ref.1, f32[192,128]{1,0:T(8,128)} %bitcast.7, s32[4,128]{1,0:T(4,128)} %bitcast.10, s32[4,128]{1,0:T(4,128)} %bitcast.11, s32[512]{0:T(512)} %src_hbm.1, bf16[128,4096]{1,0:T(8,128)(2,1)} %basis_hbm.3, f32[254,4096]{1,0:T(8,128)} %edges_hbm.3, ...), custom_call_target="tpu_custom_call" | custom-call | flops 1000000000 | bytes 12000000 | tf_op jit(solution)/shard_map/up/pallas_call | solution.py:687
  12.6 0.0 copy-start
  12.6 11.6 %all-to-all-start = ((bf16[128,80,128]{2,1,0:T(8,128)(2,1)}), bf16[128,80,128]{2,1,0:T(8,128)(2,1)}, u32[]{:S(2)}, u32[]{:S(2)}) async-start(bf16[128,80,128]{2,1,0:T(8,128)(2,1)} %bitcast.6), calls=%async_computation | async-start | bytes 5242880 | tf_op jit(solution)/shard_map/all_to_all | solution.py:798
  24.2 0.0 copy-done
  24.2 0.1 fusion
  24.3 0.0 collective-permute-start
  24.3 7.2 %collective-permute-start.1 = (bf16[16,64]{1,0:T(8,128)(2,1)S(1)}, bf16[16,64]{1,0:T(8,128)(2,1)S(1)}, u32[]{:S(2)}, u32[]{:S(2)}) collective-permute-start(bf16[16,64]{1,0:T(8,128)(2,1)S(1)} %get-tuple-element.24), channel_id=1, source_target_pairs={{1,0},{2,1},{3,2},{4,3},{5,4},{6,5},{7,6},{8,7},{9,8},{10,9},{11,1... | collective-permute-start | bytes 6152 | tf_op jit(solution)/shard_map/ppermute | solution.py:797
  31.6 0.7 %concatenate.8.xe_ref = bf16[16,8320]{1,0:T(8,128)(2,1)} pad(bf16[16,8192]{1,0:T(8,128)(2,1)S(1)} %copy-done, bf16[]{:T(256)} %constant.1.clone.1), padding=0_0x0_128 | pad | bytes 528386 | tf_op jit(solution)/shard_map/concatenate | solution.py:803
  32.3 0.9 %concatenate.7.xs_ref = bf16[16,8320]{1,0:T(8,128)(2,1)} concatenate(bf16[16,64]{1,0:T(8,128)(2,1)S(1)} %broadcast_in_dim.3, bf16[16,8192]{1,0:T(8,128)(2,1)S(1)} %copy-done, bf16[16,64]{1,0:T(8,128)(2,1)S(1)} %broadcast_in_dim.3), dimensions={1} | concatenate | bytes 532480 | tf_op jit(solution)/shard_map/concatenate | solution.py:802
  33.2 18.3 %mid.1 = (f32[16,8192]{1,0:T(8,128)}, bf16[4096,128]{1,0:T(8,128)(2,1)}, bf16[4096,128]{1,0:T(8,128)(2,1)}, bf16[7,64,128]{2,1,0:T(8,128)(2,1)}, bf16[64,128]{1,0:T(8,128)(2,1)}) custom-call(f32[8,128]{1,0:T(8,128)} %get-tuple-element.17.after_ref, bf16[16,8320]{1,0:T(8,128)(2,1)} %concatenate.7.xs_ref, bf16[16,8320]{1,0:T(8,128)(2,1)} %concatenate.8.xe_ref, ...), custom_call_target="tpu_custom_call" | custom-call | flops 1000000000 | bytes 14000000 | tf_op jit(solution)/shard_map/mid/pallas_call | solution.py:720
  51.5 7.5 %collective-permute-done.before_ref = bf16[16,64]{1,0:T(8,128)(2,1)S(1)} collective-permute-done((bf16[16,64]{1,0:T(8,128)(2,1)S(1)}, bf16[16,64]{1,0:T(8,128)(2,1)S(1)}, u32[]{:S(2)}, u32[]{:S(2)}) %collective-permute-start) | collective-permute-done | bytes 2080 | tf_op jit(solution)/shard_map/ppermute | solution.py:796
  59.0 0.0 copy-start.1
  59.0 0.0 collective-permute-done.1.following_ref
  59.0 0.0 copy-start.2
  59.0 1.0 %all-to-all-done = bf16[128,80,128]{2,1,0:T(8,128)(2,1)} async-done(((bf16[128,80,128]{2,1,0:T(8,128)(2,1)}), bf16[128,80,128]{2,1,0:T(8,128)(2,1)}, u32[]{:S(2)}, u32[]{:S(2)}) %all-to-all-start) | async-done | bytes 2621472 | tf_op jit(solution)/shard_map/all_to_all | solution.py:798
  60.1 0.0 copy-done.1
  60.1 0.0 copy-done.2
  60.1 6.4 %down.1 = f32[16,8192]{1,0:T(8,128)} custom-call(bf16[1280,8,128]{2,1,0:T(8,128)(2,1)} %bitcast.4.got_hbm, f32[16,8192]{1,0:T(8,128)} %get-tuple-element.18.near_hbm, bf16[4096,128]{1,0:T(8,128)(2,1)} %get-tuple-element.19.down_hbm, bf16[4096,128]{1,0:T(8,128)(2,1)} %get-tuple-element.20.basis_hbm, bf16[7,64,128]{2,1,0:T(8,128)(2,1)} %get-tuple-element.21.top_ref, ...), custom_call_target="tpu_custom_call" | custom-call | flops 1000000000 | bytes 8000000 | tf_op jit(solution)/shard_map/down/pallas_call | solution.py:752
  (1 shorter events, 0.0 us)
Async XLA Ops:
  12.6 11.6 %copy-start = (bf16[16,8192]{1,0:T(8,128)(2,1)S(1)}, bf16[16,8192]{1,0:T(8,128)(2,1)}, u32[]{:S(2)}) copy-start(bf16[16,8192]{1,0:T(8,128)(2,1)} %x_ref.1) | copy-start | bytes 786436
  12.6 47.5 %all-to-all-start = ((bf16[128,80,128]{2,1,0:T(8,128)(2,1)}), bf16[128,80,128]{2,1,0:T(8,128)(2,1)}, u32[]{:S(2)}, u32[]{:S(2)}) async-start(bf16[128,80,128]{2,1,0:T(8,128)(2,1)} %bitcast.6), calls=%async_computation | async-start | bytes 5242880 | tf_op jit(solution)/shard_map/all_to_all | solution.py:798
  24.3 34.7 %collective-permute-start = (bf16[16,64]{1,0:T(8,128)(2,1)S(1)}, bf16[16,64]{1,0:T(8,128)(2,1)S(1)}, u32[]{:S(2)}, u32[]{:S(2)}) collective-permute-start(bf16[16,64]{1,0:T(8,128)(2,1)S(1)} %get-tuple-element.23), channel_id=1, source_target_pairs={{0,1},{1,2},{2,3},{3,4},{4,5},{5,6},{6,7},{7,8},{8,9},{9,10},{10,1... | collective-permute-start | bytes 6152 | tf_op jit(solution)/shard_map/ppermute | solution.py:796
  24.3 34.7 %collective-permute-start.1 = (bf16[16,64]{1,0:T(8,128)(2,1)S(1)}, bf16[16,64]{1,0:T(8,128)(2,1)S(1)}, u32[]{:S(2)}, u32[]{:S(2)}) collective-permute-start(bf16[16,64]{1,0:T(8,128)(2,1)S(1)} %get-tuple-element.24), channel_id=1, source_target_pairs={{1,0},{2,1},{3,2},{4,3},{5,4},{6,5},{7,6},{8,7},{9,8},{10,9},{11,1... | collective-permute-start | bytes 6152 | tf_op jit(solution)/shard_map/ppermute | solution.py:797
  59.0 1.1 %copy-start.1 = (bf16[16,64]{1,0:T(8,128)(2,1)}, bf16[16,64]{1,0:T(8,128)(2,1)S(1)}, u32[]{:S(2)}) copy-start(bf16[16,64]{1,0:T(8,128)(2,1)S(1)} %collective-permute-done.before_ref) | copy-start | bytes 6148
  59.0 1.0 %copy-start.2 = (bf16[16,64]{1,0:T(8,128)(2,1)}, bf16[16,64]{1,0:T(8,128)(2,1)S(1)}, u32[]{:S(2)}) copy-start(bf16[16,64]{1,0:T(8,128)(2,1)S(1)} %collective-permute-done.1.following_ref) | copy-start | bytes 6148
